TPU v7x, 32 devices: a whole 2x2x4 slice. The times are simulated.
32 devices in a mesh: shard: 4 (over x, core), ctx: 8 (over z, y).
Axes of the slice: x: 2, y: 2, z: 4, core: 2. Of those that a mesh axis runs over, the one named last changes fastest.
Arguments:
- tokens: bfloat16 [2, 2048, 768], P(None, ('ctx', 'shard')), may hold values from -6 to 6
- gain_attn: float32 [768], replicated, may hold values from 0.5 to 1.5
- gain_ffn: float32 [768], replicated, may hold values from 0.5 to 1.5
- query_key_value_weight: bfloat16 [768, 2304], P('shard'), may hold values from -0.21875 to 0.21875
- attention_out_weight: bfloat16 [768, 768], P('shard'), may hold values from -6 to 6
- feedforward_in_weight: bfloat16 [768, 2304], P('shard'), may hold values from -0.21875 to 0.21875
- feedforward_out_weight: bfloat16 [1152, 768], P('shard'), may hold values from -0.1875 to 0.1875
- cotangent: bfloat16 [2, 2048, 768], P(None, ('ctx', 'shard')), may hold values from -6 to 6
Outputs:
- output: bfloat16 [2, 2048, 768], P(None, ('ctx', 'shard'))
- grad_tokens: bfloat16 [2, 2048, 768], P(None, ('ctx', 'shard'))
- grad_gain_attn: float32 [768], replicated
- grad_gain_ffn: float32 [768], replicated
- grad_w_qkv: float32 [768, 2304], P('shard')
- grad_w_attn: float32 [768, 768], P('shard')
- grad_w_in: float32 [768, 2304], P('shard')
- grad_w_out: float32 [1152, 768], P('shard')
All inputs are finite; a program needn't handle non-finite values.
Results may differ from a plain program's by a relative error of at most 0.02.
Values may be sent and summed in bfloat16 or wider, within the bound.
No kernel may reach another device: no remote copies, remote signals or barrier semaphores. Data moves between devices by JAX's collectives and lax.ppermute only.
A program may use at most 192 MiB of HBM per device.

v0:
```python
import jax
import jax.numpy as jnp
from jax import lax
from jax.sharding import PartitionSpec as P

HEADS = 12
HEAD_DIM = 64


epsilon = 1e-05
rope_base = 160000.0


def passed_along(value, axis, steps):
    count = lax.axis_size(axis)
    pairs = [(source, (source + steps) % count) for source in range(count)]
    return lax.ppermute(value, axis, pairs)


def layer_norm(values, scale_vector):
    centre = jnp.mean(values, axis=-1, keepdims=True)
    shifted = values - centre
    spread = jnp.mean(shifted * shifted, axis=-1, keepdims=True)
    return shifted * lax.rsqrt(spread + epsilon) * scale_vector


def rope_tables(positions, half_dim):
    freq_index = jnp.arange(half_dim, dtype=jnp.float32)
    inverse_freq = jnp.exp(freq_index * (-1.0 / half_dim) * jnp.log(jnp.float32(rope_base)))
    angles = positions[:, None] * inverse_freq[None, :]
    angles = jnp.concatenate([angles, angles], axis=1)
    return (jnp.cos(angles), jnp.sin(angles))


def rotate(values, cosine, sine_table, half_dim):
    turned = jnp.concatenate([-values[..., half_dim:], values[..., :half_dim]], axis=-1)
    return values * cosine[:, None, :] + turned * sine_table[:, None, :]


def unrotate(grads, cosine, sine_table, half_dim):
    primal, pullback = jax.vjp(lambda values: rotate(values, cosine, sine_table, half_dim), grads)
    return pullback(grads)[0]


def geglu(gate_up_values):
    split_at = gate_up_values.shape[-1] // 2
    return (
        jax.nn.gelu(gate_up_values[:, :split_at], approximate=False) * gate_up_values[:, split_at:]
    )


def finish_grads(grad_query, grad_kv, cosine, sine_table, half_dim):
    seq_count, block_rows, packed = grad_kv.shape
    local_heads = grad_query.shape[2]
    head_dim = grad_query.shape[3]
    grad_kv_heads = grad_kv.reshape(seq_count, block_rows, local_heads, 2, head_dim)
    grad_key_pre = unrotate(grad_kv_heads[:, :, :, 0], cosine, sine_table, half_dim)
    grad_kv_low = jnp.stack([grad_key_pre, grad_kv_heads[:, :, :, 1]], axis=3)
    grad_kv_low = grad_kv_low.reshape(seq_count, block_rows, packed).astype(jnp.bfloat16)
    grad_query_low = unrotate(grad_query, cosine, sine_table, half_dim)
    grad_query_low = grad_query_low.reshape(seq_count, block_rows, local_heads * head_dim).astype(
        jnp.bfloat16
    )
    return (grad_query_low, grad_kv_low)


def block_backward(
    query_heads, grad_att_heads, log_sum, row_delta, block_keys, block_values, score_scale
):
    seq_count, kv_rows, local_heads, head_dim = block_keys.shape
    scores = (
        jnp.einsum("sqhd,skhd->shqk", query_heads, block_keys, preferred_element_type=jnp.float32)
        * score_scale
    )
    probabilities = jnp.exp(scores - log_sum[..., None])
    grad_values = jnp.einsum(
        "shqk,sqhd->skhd",
        probabilities.astype(jnp.bfloat16),
        grad_att_heads,
        preferred_element_type=jnp.float32,
    )
    grad_probs = jnp.einsum(
        "sqhd,skhd->shqk", grad_att_heads, block_values, preferred_element_type=jnp.float32
    )
    grad_scores = (probabilities * (grad_probs - row_delta[..., None])).astype(jnp.bfloat16)
    query_term = (
        jnp.einsum("shqk,skhd->sqhd", grad_scores, block_keys, preferred_element_type=jnp.float32)
        * score_scale
    )
    grad_keys = (
        jnp.einsum("shqk,sqhd->skhd", grad_scores, query_heads, preferred_element_type=jnp.float32)
        * score_scale
    )
    update = jnp.stack([grad_keys, grad_values], axis=3).reshape(
        seq_count, kv_rows, local_heads * 2 * head_dim
    )
    return (query_term, update)


def local(
    tokens,
    gain_attn,
    gain_ffn,
    query_key_value_weight,
    attention_out_weight,
    feedforward_in_weight,
    feedforward_out_weight,
    cotangent,
):
    seq_count, row_count, features = tokens.shape
    shards = lax.axis_size("shard")
    cycle_size = lax.axis_size("ctx")
    head_count = HEADS
    head_dim = HEAD_DIM
    half_dim = head_dim // 2
    score_scale = head_dim ** (-0.5)
    tok_count = seq_count * row_count
    full_qkv, full_attn, full_in, full_out = (
        lax.all_gather(query_key_value_weight, "shard", axis=0, tiled=True),
        lax.all_gather(attention_out_weight, "shard", axis=0, tiled=True),
        lax.all_gather(feedforward_in_weight, "shard", axis=0, tiled=True),
        lax.all_gather(feedforward_out_weight, "shard", axis=0, tiled=True),
    )
    ctx_index = lax.axis_index("ctx")
    shard_index = lax.axis_index("shard")
    own_start = (ctx_index * shards + shard_index) * row_count
    own_cos, own_sin = rope_tables(
        (own_start + jnp.arange(row_count, dtype=jnp.int32)).astype(jnp.float32), half_dim
    )
    layer_input = tokens.astype(jnp.float32).reshape(tok_count, features)
    attention_normed, norm_a_pull = jax.vjp(layer_norm, layer_input, gain_attn)
    normed_a_low = attention_normed.astype(jnp.bfloat16)
    query_key_value_rows = jnp.dot(normed_a_low, full_qkv, preferred_element_type=jnp.float32)
    query_key_value_rows = query_key_value_rows.reshape(
        seq_count, row_count, 3, head_count, head_dim
    )
    queries = rotate(query_key_value_rows[:, :, 0], own_cos, own_sin, half_dim).astype(jnp.bfloat16)
    key_rows = rotate(query_key_value_rows[:, :, 1], own_cos, own_sin, half_dim).astype(
        jnp.bfloat16
    )
    value_rows = query_key_value_rows[:, :, 2].astype(jnp.bfloat16)
    kv_local = jnp.stack([key_rows, value_rows], axis=3).reshape(
        seq_count, row_count, head_count * 2 * head_dim
    )
    query_flat = queries.reshape(seq_count, row_count, features)
    kv_block = lax.all_gather(kv_local, "shard", axis=1, tiled=True)
    local_heads = query_flat.shape[2] // head_dim
    query_rows = query_flat.shape[1]
    kv_rows = kv_block.shape[1]
    query_heads = query_flat.reshape(seq_count, query_rows, local_heads, head_dim)

    def key_block(key_piece, offset):
        kv_part = lax.dynamic_slice_in_dim(key_piece, offset, kv_rows, 1)
        kv_part = kv_part.reshape(seq_count, kv_rows, local_heads, 2, head_dim)
        return (kv_part[:, :, :, 0], kv_part[:, :, :, 1])

    start_state = (
        jnp.full((seq_count, local_heads, query_rows), -1e30, jnp.float32),
        jnp.zeros((seq_count, local_heads, query_rows), jnp.float32),
        jnp.zeros((seq_count, local_heads, query_rows, head_dim), jnp.float32),
    )
    key_piece = lax.all_gather(kv_block, "ctx", axis=1, tiled=True)

    def one_block(block_index, running):
        row_max, row_sum, accum = running
        block_keys, block_values = key_block(key_piece, block_index * kv_rows)
        scores = (
            jnp.einsum(
                "sqhd,skhd->shqk", query_heads, block_keys, preferred_element_type=jnp.float32
            )
            * score_scale
        )
        new_max = jnp.maximum(row_max, jnp.max(scores, axis=-1))
        weights = jnp.exp(scores - new_max[..., None])
        factor = jnp.exp(row_max - new_max)
        row_sum = row_sum * factor + jnp.sum(weights, axis=-1)
        accum = accum * factor[..., None] + jnp.einsum(
            "shqk,skhd->shqd",
            weights.astype(jnp.bfloat16),
            block_values,
            preferred_element_type=jnp.float32,
        )
        return (new_max, row_sum, accum)

    row_max, row_sum, accum = lax.fori_loop(
        0, key_piece.shape[1] // kv_rows, one_block, start_state
    )
    log_sum = row_max + jnp.log(row_sum)
    attention_result = accum / row_sum[..., None]
    attended_low = (
        attention_result.transpose(0, 2, 1, 3)
        .reshape(seq_count, query_rows, local_heads * head_dim)
        .astype(jnp.bfloat16)
    )
    attended_flat = attended_low.reshape(tok_count, features)
    residual_middle = layer_input + jnp.dot(
        attended_flat, full_attn, preferred_element_type=jnp.float32
    )
    feedforward_normed, norm_f_pull = jax.vjp(layer_norm, residual_middle, gain_ffn)
    normed_f_low = feedforward_normed.astype(jnp.bfloat16)
    gate_up_values = jnp.dot(normed_f_low, full_in, preferred_element_type=jnp.float32)
    hidden_activation, geglu_pull = jax.vjp(geglu, gate_up_values)
    hidden_low = hidden_activation.astype(jnp.bfloat16)
    output = (
        residual_middle + jnp.dot(hidden_low, full_out, preferred_element_type=jnp.float32)
    ).astype(jnp.bfloat16)
    output = output.reshape(seq_count, row_count, features)
    grad_out = cotangent.reshape(tok_count, features)
    grad_hidden = jnp.einsum("nd,fd->nf", grad_out, full_out, preferred_element_type=jnp.float32)
    grad_gate_up = geglu_pull(grad_hidden)[0].astype(jnp.bfloat16)
    grad_normed_f = jnp.einsum(
        "ne,de->nd", grad_gate_up, full_in, preferred_element_type=jnp.float32
    )
    grad_middle_norm, grad_gain_ffn = norm_f_pull(grad_normed_f)
    grad_middle = grad_out.astype(jnp.float32) + grad_middle_norm
    grad_branch = grad_middle.astype(jnp.bfloat16)
    grad_attended = jnp.einsum(
        "nd,fd->nf", grad_branch, full_attn, preferred_element_type=jnp.float32
    )
    grad_attended = grad_attended.astype(jnp.bfloat16).reshape(seq_count, row_count, features)
    grad_att_heads = grad_attended.reshape(seq_count, query_rows, local_heads, head_dim)
    row_delta = jnp.sum(
        grad_att_heads.transpose(0, 2, 1, 3).astype(jnp.float32) * attention_result, axis=-1
    )

    def back_block(turn_index, running):
        moving, grad_moving, grad_query = running
        block_keys, block_values = key_block(moving, 0)
        query_term, update = block_backward(
            query_heads, grad_att_heads, log_sum, row_delta, block_keys, block_values, score_scale
        )
        grad_query = grad_query + query_term
        moving = passed_along(moving, "ctx", 1)
        grad_moving = passed_along((grad_moving + update).astype(jnp.bfloat16), "ctx", 1).astype(
            jnp.float32
        )
        return (moving, grad_moving, grad_query)

    back_state = (
        kv_block,
        jnp.zeros(kv_block.shape, jnp.float32),
        jnp.zeros((seq_count, query_rows, local_heads, head_dim), jnp.float32),
    )
    home_block, grad_kv, grad_query = lax.fori_loop(0, cycle_size, back_block, back_state)
    grad_kv_sum = lax.psum_scatter(
        grad_kv.astype(jnp.bfloat16), "shard", scatter_dimension=1, tiled=True
    ).astype(jnp.float32)
    grad_query_tok, grad_kv_tok = finish_grads(grad_query, grad_kv_sum, own_cos, own_sin, half_dim)
    grad_kv_split = grad_kv_tok.reshape(tok_count, head_count, 2, head_dim)
    grad_qkv = jnp.concatenate(
        [
            grad_query_tok.reshape(tok_count, features),
            grad_kv_split[:, :, 0].reshape(tok_count, features),
            grad_kv_split[:, :, 1].reshape(tok_count, features),
        ],
        axis=1,
    )
    grad_normed_a = jnp.einsum("ne,de->nd", grad_qkv, full_qkv, preferred_element_type=jnp.float32)
    grad_inputs_norm, grad_gain_attn = norm_a_pull(grad_normed_a)
    grad_tokens = (
        (grad_middle + grad_inputs_norm)
        .astype(jnp.bfloat16)
        .reshape(seq_count, row_count, features)
    )
    wide_part = lax.psum_scatter(
        jnp.concatenate(
            [
                jnp.einsum("nd,ne->de", normed_a_low, grad_qkv, preferred_element_type=jnp.float32),
                jnp.einsum(
                    "nd,ne->de", attended_flat, grad_branch, preferred_element_type=jnp.float32
                ),
                jnp.einsum(
                    "nd,ne->de", normed_f_low, grad_gate_up, preferred_element_type=jnp.float32
                ),
            ],
            axis=1,
        ).astype(jnp.bfloat16),
        "shard",
        scatter_dimension=0,
        tiled=True,
    ).astype(jnp.float32)
    gain_terms = jnp.broadcast_to(
        jnp.concatenate([grad_gain_attn, grad_gain_ffn])[None, :], (shards, 2 * features)
    )
    out_term = jnp.einsum("nf,nd->fd", hidden_low, grad_out, preferred_element_type=jnp.float32)
    out_part, gain_part = (
        lax.psum_scatter(
            out_term.astype(jnp.bfloat16), "shard", scatter_dimension=0, tiled=True
        ).astype(jnp.float32),
        lax.psum_scatter(
            gain_terms.astype(jnp.bfloat16), "shard", scatter_dimension=0, tiled=True
        ).astype(jnp.float32),
    )
    wide_sum, out_sum, gain_sum = lax.psum((wide_part, out_part, gain_part), "ctx")
    qkv_cols = 3 * features
    return (
        output,
        grad_tokens,
        gain_sum[0, :features],
        gain_sum[0, features:],
        wide_sum[:, :qkv_cols],
        wide_sum[:, qkv_cols : qkv_cols + features],
        wide_sum[:, qkv_cols + features :],
        out_sum,
    )


def solution(mesh):
    return jax.shard_map(
        local,
        mesh=mesh,
        in_specs=(
            P(None, ("ctx", "shard"), None),
            P(),
            P(),
            P("shard", None),
            P("shard", None),
            P("shard", None),
            P("shard", None),
            P(None, ("ctx", "shard"), None),
        ),
        out_specs=(
            P(None, ("ctx", "shard"), None),
            P(None, ("ctx", "shard"), None),
            P(),
            P(),
            P("shard", None),
            P("shard", None),
            P("shard", None),
            P("shard", None),
        ),
        check_vma=False,
    )
```

profile of v0, /device:TPU:0, one launch (start us, length us, event | category | flops | bytes accessed | tf_op | source)
XLA Modules:
  0.0 1338.5 jit_solution(17989844202012323229)
XLA Ops:
  10.4 32.7 %all-gather.7.cloned.1.call-done = bf16[768,2304]{1,0:T(8,128)(2,1)} async-done(((bf16[192,2304]{1,0:T(8,128)(2,1)}), bf16[768,2304]{1,0:T(8,128)(2,1)}) %all-gather.7.cloned.1.call-update) | async-done | bytes 3538960 | tf_op jit(solution)/shard_map/all_gather | solution.py:119
  43.0 5.8 copy.58
  58.7 19.7 %all-gather.9.cloned.1.call-done = bf16[2,256,1536]{2,1,0:T(8,128)(2,1)} async-done(((bf16[2,64,1536]{2,1,0:T(8,128)(2,1)}), bf16[2,256,1536]{2,1,0:T(8,128)(2,1)}) %all-gather.9.cloned.1.call-update) | async-done | bytes 1572880 | tf_op jit(solution)/shard_map/all_gather | solution.py:146
  87.3 169.6 %all-gather.11.cloned.1.call-done = bf16[2,2048,1536]{2,1,0:T(8,128)(2,1)} async-done(((bf16[2,256,1536]{2,1,0:T(8,128)(2,1)}), bf16[2,2048,1536]{2,1,0:T(8,128)(2,1)}) %all-gather.11.cloned.1.call-update) | async-done | bytes 12582928 | tf_op jit(solution)/shard_map/all_gather | solution.py:162
  256.8 64.5 %while.33 = (s32[]{:T(128)}, f32[2,12,64]{2,1,0:T(8,128)S(1)}, f32[2,12,64]{2,1,0:T(8,128)}, f32[2,12,64,64]{3,2,1,0:T(8,128)}, bf16[2,2048,1536]{2,1,0:T(8,128)...) while((s32[]{:T(128)}, f32[2,12,64]{2,1,0:T(8,128)S(1)}, ...), condition=%wide.region_5.0_spmd.clone, body=%wide.region_2.0_spmd.clone.sunk | while | flops 103325184 | bytes 17273108 | solution.py:185
  340.0 633.2 %while.34 = (s32[]{:T(128)}, bf16[2,256,1536]{1,2,0:T(8,128)(2,1)S(1)}, f32[2,256,1536]{1,2,0:T(8,128)}, f32[2,64,12,64]{3,1,2,0:T(8,128)}, bf16[2,64,12,64]{1,3...) while((s32[]{:T(128)}, ...), condition=%wide.region_12.0_spmd.clone, body=%wide.region_11.0_spmd.clone.sunk | while | flops 258637824 | bytes 60273024 | solution.py:244
  352.7 36.2 %collective-permute-done.1 = bf16[2,256,1536]{1,2,0:T(8,128)(2,1)} collective-permute-done((bf16[2,256,1536]{1,2,0:T(8,128)(2,1)}, bf16[2,256,1536]{1,2,0:T(8,128)(2,1)}, u32[]{:S(2)}, u32[]{:S(2)}) %collective-permute-start.1) | collective-permute-done | bytes 1572896 | tf_op jit(solution)/shard_map/while/body/eval_jaxpr/ppermute | solution.py:17
  392.3 28.2 %collective-permute-done = bf16[2,256,1536]{1,2,0:T(8,128)(2,1)S(1)} collective-permute-done((bf16[2,256,1536]{1,2,0:T(8,128)(2,1)}, bf16[2,256,1536]{1,2,0:T(8,128)(2,1)S(1)}, u32[]{:S(2)}, u32[]{:S(2)}) %collective-permute-start) | collective-permute-done | bytes 1572896 | tf_op jit(solution)/shard_map/while/body/eval_jaxpr/ppermute | solution.py:17
  427.3 3.7 fusion.103
  434.8 36.5 %collective-permute-done.1 = bf16[2,256,1536]{1,2,0:T(8,128)(2,1)} collective-permute-done((bf16[2,256,1536]{1,2,0:T(8,128)(2,1)}, bf16[2,256,1536]{1,2,0:T(8,128)(2,1)}, u32[]{:S(2)}, u32[]{:S(2)}) %collective-permute-start.1) | collective-permute-done | bytes 1572896 | tf_op jit(solution)/shard_map/while/body/eval_jaxpr/ppermute | solution.py:17
  474.6 27.4 %collective-permute-done = bf16[2,256,1536]{1,2,0:T(8,128)(2,1)S(1)} collective-permute-done((bf16[2,256,1536]{1,2,0:T(8,128)(2,1)}, bf16[2,256,1536]{1,2,0:T(8,128)(2,1)S(1)}, u32[]{:S(2)}, u32[]{:S(2)}) %collective-permute-start) | collective-permute-done | bytes 1572896 | tf_op jit(solution)/shard_map/while/body/eval_jaxpr/ppermute | solution.py:17
  508.8 3.7 fusion.103
  515.8 37.0 %collective-permute-done.1 = bf16[2,256,1536]{1,2,0:T(8,128)(2,1)} collective-permute-done((bf16[2,256,1536]{1,2,0:T(8,128)(2,1)}, bf16[2,256,1536]{1,2,0:T(8,128)(2,1)}, u32[]{:S(2)}, u32[]{:S(2)}) %collective-permute-start.1) | collective-permute-done | bytes 1572896 | tf_op jit(solution)/shard_map/while/body/eval_jaxpr/ppermute | solution.py:17
  556.2 26.5 %collective-permute-done = bf16[2,256,1536]{1,2,0:T(8,128)(2,1)S(1)} collective-permute-done((bf16[2,256,1536]{1,2,0:T(8,128)(2,1)}, bf16[2,256,1536]{1,2,0:T(8,128)(2,1)S(1)}, u32[]{:S(2)}, u32[]{:S(2)}) %collective-permute-start) | collective-permute-done | bytes 1572896 | tf_op jit(solution)/shard_map/while/body/eval_jaxpr/ppermute | solution.py:17
  589.5 3.7 fusion.103
  596.1 37.4 %collective-permute-done.1 = bf16[2,256,1536]{1,2,0:T(8,128)(2,1)} collective-permute-done((bf16[2,256,1536]{1,2,0:T(8,128)(2,1)}, bf16[2,256,1536]{1,2,0:T(8,128)(2,1)}, u32[]{:S(2)}, u32[]{:S(2)}) %collective-permute-start.1) | collective-permute-done | bytes 1572896 | tf_op jit(solution)/shard_map/while/body/eval_jaxpr/ppermute | solution.py:17
  636.8 25.7 %collective-permute-done = bf16[2,256,1536]{1,2,0:T(8,128)(2,1)S(1)} collective-permute-done((bf16[2,256,1536]{1,2,0:T(8,128)(2,1)}, bf16[2,256,1536]{1,2,0:T(8,128)(2,1)S(1)}, u32[]{:S(2)}, u32[]{:S(2)}) %collective-permute-start) | collective-permute-done | bytes 1572896 | tf_op jit(solution)/shard_map/while/body/eval_jaxpr/ppermute | solution.py:17
  675.9 37.4 %collective-permute-done.1 = bf16[2,256,1536]{1,2,0:T(8,128)(2,1)} collective-permute-done((bf16[2,256,1536]{1,2,0:T(8,128)(2,1)}, bf16[2,256,1536]{1,2,0:T(8,128)(2,1)}, u32[]{:S(2)}, u32[]{:S(2)}) %collective-permute-start.1) | collective-permute-done | bytes 1572896 | tf_op jit(solution)/shard_map/while/body/eval_jaxpr/ppermute | solution.py:17
  716.6 24.8 %collective-permute-done = bf16[2,256,1536]{1,2,0:T(8,128)(2,1)S(1)} collective-permute-done((bf16[2,256,1536]{1,2,0:T(8,128)(2,1)}, bf16[2,256,1536]{1,2,0:T(8,128)(2,1)S(1)}, u32[]{:S(2)}, u32[]{:S(2)}) %collective-permute-start) | collective-permute-done | bytes 1572896 | tf_op jit(solution)/shard_map/while/body/eval_jaxpr/ppermute | solution.py:17
  754.8 37.4 %collective-permute-done.1 = bf16[2,256,1536]{1,2,0:T(8,128)(2,1)} collective-permute-done((bf16[2,256,1536]{1,2,0:T(8,128)(2,1)}, bf16[2,256,1536]{1,2,0:T(8,128)(2,1)}, u32[]{:S(2)}, u32[]{:S(2)}) %collective-permute-start.1) | collective-permute-done | bytes 1572896 | tf_op jit(solution)/shard_map/while/body/eval_jaxpr/ppermute | solution.py:17
  795.6 23.9 %collective-permute-done = bf16[2,256,1536]{1,2,0:T(8,128)(2,1)S(1)} collective-permute-done((bf16[2,256,1536]{1,2,0:T(8,128)(2,1)}, bf16[2,256,1536]{1,2,0:T(8,128)(2,1)S(1)}, u32[]{:S(2)}, u32[]{:S(2)}) %collective-permute-start) | collective-permute-done | bytes 1572896 | tf_op jit(solution)/shard_map/while/body/eval_jaxpr/ppermute | solution.py:17
  832.9 37.4 %collective-permute-done.1 = bf16[2,256,1536]{1,2,0:T(8,128)(2,1)} collective-permute-done((bf16[2,256,1536]{1,2,0:T(8,128)(2,1)}, bf16[2,256,1536]{1,2,0:T(8,128)(2,1)}, u32[]{:S(2)}, u32[]{:S(2)}) %collective-permute-start.1) | collective-permute-done | bytes 1572896 | tf_op jit(solution)/shard_map/while/body/eval_jaxpr/ppermute | solution.py:17
  873.7 23.1 %collective-permute-done = bf16[2,256,1536]{1,2,0:T(8,128)(2,1)S(1)} collective-permute-done((bf16[2,256,1536]{1,2,0:T(8,128)(2,1)}, bf16[2,256,1536]{1,2,0:T(8,128)(2,1)S(1)}, u32[]{:S(2)}, u32[]{:S(2)}) %collective-permute-start) | collective-permute-done | bytes 1572896 | tf_op jit(solution)/shard_map/while/body/eval_jaxpr/ppermute | solution.py:17
  910.2 37.4 %collective-permute-done.1 = bf16[2,256,1536]{1,2,0:T(8,128)(2,1)} collective-permute-done((bf16[2,256,1536]{1,2,0:T(8,128)(2,1)}, bf16[2,256,1536]{1,2,0:T(8,128)(2,1)}, u32[]{:S(2)}, u32[]{:S(2)}) %collective-permute-start.1) | collective-permute-done | bytes 1572896 | tf_op jit(solution)/shard_map/while/body/eval_jaxpr/ppermute | solution.py:17
  950.9 22.2 %collective-permute-done = bf16[2,256,1536]{1,2,0:T(8,128)(2,1)S(1)} collective-permute-done((bf16[2,256,1536]{1,2,0:T(8,128)(2,1)}, bf16[2,256,1536]{1,2,0:T(8,128)(2,1)S(1)}, u32[]{:S(2)}, u32[]{:S(2)}) %collective-permute-start) | collective-permute-done | bytes 1572896 | tf_op jit(solution)/shard_map/while/body/eval_jaxpr/ppermute | solution.py:17
  973.2 5.5 copy.72
  983.5 4.0 convolution_convert_fusion
  987.8 32.5 %all-reduce.12.cloned.1.call-done = bf16[2,256,1536]{2,0,1:T(2,128)(2,1)} async-done(((bf16[2,256,1536]{2,0,1:T(2,128)(2,1)}), bf16[2,256,1536]{2,0,1:T(2,128)(2,1)}) %all-reduce.12.cloned.1.call-update) | async-done | bytes 1572880
  1049.1 10.3 all-reduce.7
  1060.0 66.0 %reduce-scatter.3.cloned.1.call-done = bf16[192,5376]{1,0:T(8,128)(2,1)} async-done(((bf16[768,5376]{1,0:T(8,128)(2,1)}), bf16[192,5376]{1,0:T(8,128)(2,1)}) %reduce-scatter.3.cloned.1.call-update) | async-done | bytes 2064400 | tf_op jit(solution)/shard_map/reduce_scatter | solution.py:265
  1126.0 199.5 %all-reduce.13 = (f32[1,1536]{1,0:T(1,128)S(1)}, f32[192,5376]{1,0:T(8,128)}, f32[288,768]{1,0:T(8,128)}) all-reduce(f32[1,1536]{1,0:T(1,128)S(1)} %dynamic-slice_convert_fusion, bf16[192,5376]{1,0:T(8,128)(2,1)} %reduce-scatter.3.cloned.1.call-done, ...), channel_id=1, replica_groups=mesh['shard'=4,'ctx'=8] {'ctx'}, use_global_device_ids=true, to_apply=%region_19.0 | all-reduce | flops 1254912 | bytes 7532544 | tf_op jit(solution)/shard_map/psum | solution.py:294
  1325.5 4.0 fusion.50
  (538 shorter events, 262.5 us)
Async XLA Ops:
  7.2 35.9 %all-gather.7.cloned.1.call-start = ((), (), s32[]{:S(2)}) async-start(), calls=%async_computation.2 | async-start | bytes 4423680 | tf_op jit(solution)/shard_map/all_gather | solution.py:119
  7.9 70.6 %all-gather.9.cloned.1.call-start = ((), (), s32[]{:S(2)}) async-start(), calls=%async_computation.3 | async-start | bytes 1966080 | tf_op jit(solution)/shard_map/all_gather | solution.py:146
  58.7 198.1 %all-gather.11.cloned.1.call-start = ((), (), s32[]{:S(2)}) async-start(), calls=%async_computation.4 | async-start | bytes 14155776 | tf_op jit(solution)/shard_map/all_gather | solution.py:162
  78.5 245.7 %all-gather.13.cloned.1.call-start = ((), (), s32[]{:S(2)}) async-start(), calls=%async_computation.5 | async-start | bytes 1474560 | tf_op jit(solution)/shard_map/all_gather | solution.py:120
  79.1 247.8 %all-gather.15.cloned.1.call-start = ((), (), s32[]{:S(2)}) async-start(), calls=%async_computation.6 | async-start | bytes 4423680 | tf_op jit(solution)/shard_map/all_gather | solution.py:121
  79.7 250.0 %all-gather.17.cloned.1.call-start = ((), (), s32[]{:S(2)}) async-start(), calls=%async_computation.7 | async-start | bytes 2211840 | tf_op jit(solution)/shard_map/all_gather | solution.py:122
  80.3 940.0 %all-reduce.12.cloned.1.call-start = ((), (), s32[]{:S(2)}) async-start(), calls=%async_computation.10 | async-start | bytes 3145728
  348.6 40.3 %collective-permute-start.1 = (bf16[2,256,1536]{1,2,0:T(8,128)(2,1)}, bf16[2,256,1536]{1,2,0:T(8,128)(2,1)}, u32[]{:S(2)}, u32[]{:S(2)}) collective-permute-start(bf16[2,256,1536]{1,2,0:T(8,128)(2,1)} %fusion.103), channel_id=1, source_target_pairs={{0,1},{1,2},{2,3},{3,4},{4,5},{5,6},{6,7},{7,0},{8,9},{9,10},{10,1... | collective-permute-start | bytes 4718600 | tf_op jit(solution)/shard_map/while/body/eval_jaxpr/ppermute | solution.py:17
  349.0 71.5 %collective-permute-start = (bf16[2,256,1536]{1,2,0:T(8,128)(2,1)}, bf16[2,256,1536]{1,2,0:T(8,128)(2,1)S(1)}, u32[]{:S(2)}, u32[]{:S(2)}) collective-permute-start(bf16[2,256,1536]{1,2,0:T(8,128)(2,1)} %copy.111), channel_id=1, source_target_pairs={{0,1},{1,2},{2,3},{3,4},{4,5},{5,6},{6,7},{7,0},{8,9},{9,10},{10,1... | collective-permute-start | bytes 4718600 | tf_op jit(solution)/shard_map/while/body/eval_jaxpr/ppermute | solution.py:17
  352.7 67.8 %copy-start.3 = (bf16[2,64,12,64]{1,3,2,0:T(8,128)(2,1)S(1)}, bf16[2,64,12,64]{1,3,2,0:T(8,128)(2,1)}, u32[]{:S(2)}) copy-start(bf16[2,64,12,64]{1,3,2,0:T(8,128)(2,1)} %copy-done.2) | copy-start | bytes 589828 | tf_op jit(solution)/shard_map/while
  352.7 67.8 %copy-start.37 = (f32[2,12,64]{2,1,0:T(8,128)S(1)}, f32[2,12,64]{2,1,0:T(8,128)}, u32[]{:S(2)}) copy-start(f32[2,12,64]{2,1,0:T(8,128)} %copy-done.36) | copy-start | bytes 18436 | tf_op jit(solution)/shard_map/while
  352.7 67.8 %copy-start.39 = (f32[2,12,64]{2,1,0:T(8,128)S(1)}, f32[2,12,64]{2,1,0:T(8,128)}, u32[]{:S(2)}) copy-start(f32[2,12,64]{2,1,0:T(8,128)} %copy-done.38) | copy-start | bytes 18436 | tf_op jit(solution)/shard_map/while
  431.0 40.3 %collective-permute-start.1 = (bf16[2,256,1536]{1,2,0:T(8,128)(2,1)}, bf16[2,256,1536]{1,2,0:T(8,128)(2,1)}, u32[]{:S(2)}, u32[]{:S(2)}) collective-permute-start(bf16[2,256,1536]{1,2,0:T(8,128)(2,1)} %fusion.103), channel_id=1, source_target_pairs={{0,1},{1,2},{2,3},{3,4},{4,5},{5,6},{6,7},{7,0},{8,9},{9,10},{10,1... | collective-permute-start | bytes 4718600 | tf_op jit(solution)/shard_map/while/body/eval_jaxpr/ppermute | solution.py:17
  431.0 71.0 %collective-permute-start = (bf16[2,256,1536]{1,2,0:T(8,128)(2,1)}, bf16[2,256,1536]{1,2,0:T(8,128)(2,1)S(1)}, u32[]{:S(2)}, u32[]{:S(2)}) collective-permute-start(bf16[2,256,1536]{1,2,0:T(8,128)(2,1)} %copy.111), channel_id=1, source_target_pairs={{0,1},{1,2},{2,3},{3,4},{4,5},{5,6},{6,7},{7,0},{8,9},{9,10},{10,1... | collective-permute-start | bytes 4718600 | tf_op jit(solution)/shard_map/while/body/eval_jaxpr/ppermute | solution.py:17
  434.8 67.2 %copy-start.3 = (bf16[2,64,12,64]{1,3,2,0:T(8,128)(2,1)S(1)}, bf16[2,64,12,64]{1,3,2,0:T(8,128)(2,1)}, u32[]{:S(2)}) copy-start(bf16[2,64,12,64]{1,3,2,0:T(8,128)(2,1)} %copy-done.2) | copy-start | bytes 589828 | tf_op jit(solution)/shard_map/while
  434.8 67.2 %copy-start.37 = (f32[2,12,64]{2,1,0:T(8,128)S(1)}, f32[2,12,64]{2,1,0:T(8,128)}, u32[]{:S(2)}) copy-start(f32[2,12,64]{2,1,0:T(8,128)} %copy-done.36) | copy-start | bytes 18436 | tf_op jit(solution)/shard_map/while
  434.8 67.2 %copy-start.39 = (f32[2,12,64]{2,1,0:T(8,128)S(1)}, f32[2,12,64]{2,1,0:T(8,128)}, u32[]{:S(2)}) copy-start(f32[2,12,64]{2,1,0:T(8,128)} %copy-done.38) | copy-start | bytes 18436 | tf_op jit(solution)/shard_map/while
  512.5 40.3 %collective-permute-start.1 = (bf16[2,256,1536]{1,2,0:T(8,128)(2,1)}, bf16[2,256,1536]{1,2,0:T(8,128)(2,1)}, u32[]{:S(2)}, u32[]{:S(2)}) collective-permute-start(bf16[2,256,1536]{1,2,0:T(8,128)(2,1)} %fusion.103), channel_id=1, source_target_pairs={{0,1},{1,2},{2,3},{3,4},{4,5},{5,6},{6,7},{7,0},{8,9},{9,10},{10,1... | collective-permute-start | bytes 4718600 | tf_op jit(solution)/shard_map/while/body/eval_jaxpr/ppermute | solution.py:17
  512.5 70.1 %collective-permute-start = (bf16[2,256,1536]{1,2,0:T(8,128)(2,1)}, bf16[2,256,1536]{1,2,0:T(8,128)(2,1)S(1)}, u32[]{:S(2)}, u32[]{:S(2)}) collective-permute-start(bf16[2,256,1536]{1,2,0:T(8,128)(2,1)} %copy.111), channel_id=1, source_target_pairs={{0,1},{1,2},{2,3},{3,4},{4,5},{5,6},{6,7},{7,0},{8,9},{9,10},{10,1... | collective-permute-start | bytes 4718600 | tf_op jit(solution)/shard_map/while/body/eval_jaxpr/ppermute | solution.py:17
  515.8 66.8 %copy-start.39 = (f32[2,12,64]{2,1,0:T(8,128)S(1)}, f32[2,12,64]{2,1,0:T(8,128)}, u32[]{:S(2)}) copy-start(f32[2,12,64]{2,1,0:T(8,128)} %copy-done.38) | copy-start | bytes 18436 | tf_op jit(solution)/shard_map/while
  593.2 40.3 %collective-permute-start.1 = (bf16[2,256,1536]{1,2,0:T(8,128)(2,1)}, bf16[2,256,1536]{1,2,0:T(8,128)(2,1)}, u32[]{:S(2)}, u32[]{:S(2)}) collective-permute-start(bf16[2,256,1536]{1,2,0:T(8,128)(2,1)} %fusion.103), channel_id=1, source_target_pairs={{0,1},{1,2},{2,3},{3,4},{4,5},{5,6},{6,7},{7,0},{8,9},{9,10},{10,1... | collective-permute-start | bytes 4718600 | tf_op jit(solution)/shard_map/while/body/eval_jaxpr/ppermute | solution.py:17
  593.2 69.3 %collective-permute-start = (bf16[2,256,1536]{1,2,0:T(8,128)(2,1)}, bf16[2,256,1536]{1,2,0:T(8,128)(2,1)S(1)}, u32[]{:S(2)}, u32[]{:S(2)}) collective-permute-start(bf16[2,256,1536]{1,2,0:T(8,128)(2,1)} %copy.111), channel_id=1, source_target_pairs={{0,1},{1,2},{2,3},{3,4},{4,5},{5,6},{6,7},{7,0},{8,9},{9,10},{10,1... | collective-permute-start | bytes 4718600 | tf_op jit(solution)/shard_map/while/body/eval_jaxpr/ppermute | solution.py:17
  673.0 40.3 %collective-permute-start.1 = (bf16[2,256,1536]{1,2,0:T(8,128)(2,1)}, bf16[2,256,1536]{1,2,0:T(8,128)(2,1)}, u32[]{:S(2)}, u32[]{:S(2)}) collective-permute-start(bf16[2,256,1536]{1,2,0:T(8,128)(2,1)} %fusion.103), channel_id=1, source_target_pairs={{0,1},{1,2},{2,3},{3,4},{4,5},{5,6},{6,7},{7,0},{8,9},{9,10},{10,1... | collective-permute-start | bytes 4718600 | tf_op jit(solution)/shard_map/while/body/eval_jaxpr/ppermute | solution.py:17
  673.0 68.4 %collective-permute-start = (bf16[2,256,1536]{1,2,0:T(8,128)(2,1)}, bf16[2,256,1536]{1,2,0:T(8,128)(2,1)S(1)}, u32[]{:S(2)}, u32[]{:S(2)}) collective-permute-start(bf16[2,256,1536]{1,2,0:T(8,128)(2,1)} %copy.111), channel_id=1, source_target_pairs={{0,1},{1,2},{2,3},{3,4},{4,5},{5,6},{6,7},{7,0},{8,9},{9,10},{10,1... | collective-permute-start | bytes 4718600 | tf_op jit(solution)/shard_map/while/body/eval_jaxpr/ppermute | solution.py:17
  752.0 40.3 %collective-permute-start.1 = (bf16[2,256,1536]{1,2,0:T(8,128)(2,1)}, bf16[2,256,1536]{1,2,0:T(8,128)(2,1)}, u32[]{:S(2)}, u32[]{:S(2)}) collective-permute-start(bf16[2,256,1536]{1,2,0:T(8,128)(2,1)} %fusion.103), channel_id=1, source_target_pairs={{0,1},{1,2},{2,3},{3,4},{4,5},{5,6},{6,7},{7,0},{8,9},{9,10},{10,1... | collective-permute-start | bytes 4718600 | tf_op jit(solution)/shard_map/while/body/eval_jaxpr/ppermute | solution.py:17
  752.0 67.6 %collective-permute-start = (bf16[2,256,1536]{1,2,0:T(8,128)(2,1)}, bf16[2,256,1536]{1,2,0:T(8,128)(2,1)S(1)}, u32[]{:S(2)}, u32[]{:S(2)}) collective-permute-start(bf16[2,256,1536]{1,2,0:T(8,128)(2,1)} %copy.111), channel_id=1, source_target_pairs={{0,1},{1,2},{2,3},{3,4},{4,5},{5,6},{6,7},{7,0},{8,9},{9,10},{10,1... | collective-permute-start | bytes 4718600 | tf_op jit(solution)/shard_map/while/body/eval_jaxpr/ppermute | solution.py:17
  830.1 40.3 %collective-permute-start.1 = (bf16[2,256,1536]{1,2,0:T(8,128)(2,1)}, bf16[2,256,1536]{1,2,0:T(8,128)(2,1)}, u32[]{:S(2)}, u32[]{:S(2)}) collective-permute-start(bf16[2,256,1536]{1,2,0:T(8,128)(2,1)} %fusion.103), channel_id=1, source_target_pairs={{0,1},{1,2},{2,3},{3,4},{4,5},{5,6},{6,7},{7,0},{8,9},{9,10},{10,1... | collective-permute-start | bytes 4718600 | tf_op jit(solution)/shard_map/while/body/eval_jaxpr/ppermute | solution.py:17
  830.1 66.7 %collective-permute-start = (bf16[2,256,1536]{1,2,0:T(8,128)(2,1)}, bf16[2,256,1536]{1,2,0:T(8,128)(2,1)S(1)}, u32[]{:S(2)}, u32[]{:S(2)}) collective-permute-start(bf16[2,256,1536]{1,2,0:T(8,128)(2,1)} %copy.111), channel_id=1, source_target_pairs={{0,1},{1,2},{2,3},{3,4},{4,5},{5,6},{6,7},{7,0},{8,9},{9,10},{10,1... | collective-permute-start | bytes 4718600 | tf_op jit(solution)/shard_map/while/body/eval_jaxpr/ppermute | solution.py:17
  907.3 40.3 %collective-permute-start.1 = (bf16[2,256,1536]{1,2,0:T(8,128)(2,1)}, bf16[2,256,1536]{1,2,0:T(8,128)(2,1)}, u32[]{:S(2)}, u32[]{:S(2)}) collective-permute-start(bf16[2,256,1536]{1,2,0:T(8,128)(2,1)} %fusion.103), channel_id=1, source_target_pairs={{0,1},{1,2},{2,3},{3,4},{4,5},{5,6},{6,7},{7,0},{8,9},{9,10},{10,1... | collective-permute-start | bytes 4718600 | tf_op jit(solution)/shard_map/while/body/eval_jaxpr/ppermute | solution.py:17
  907.3 65.8 %collective-permute-start = (bf16[2,256,1536]{1,2,0:T(8,128)(2,1)}, bf16[2,256,1536]{1,2,0:T(8,128)(2,1)S(1)}, u32[]{:S(2)}, u32[]{:S(2)}) collective-permute-start(bf16[2,256,1536]{1,2,0:T(8,128)(2,1)} %copy.111), channel_id=1, source_target_pairs={{0,1},{1,2},{2,3},{3,4},{4,5},{5,6},{6,7},{7,0},{8,9},{9,10},{10,1... | collective-permute-start | bytes 4718600 | tf_op jit(solution)/shard_map/while/body/eval_jaxpr/ppermute | solution.py:17
  978.7 81.3 %reduce-scatter.5.cloned.1.call-start = ((), (), s32[]{:S(2)}) async-start(), calls=%async_computation.9 | async-start | bytes 2211840 | tf_op jit(solution)/shard_map/reduce_scatter | solution.py:287
  987.6 138.4 %reduce-scatter.3.cloned.1.call-start = ((), (), s32[]{:S(2)}) async-start(), calls=%async_computation.8 | async-start | bytes 10321920 | tf_op jit(solution)/shard_map/reduce_scatter | solution.py:265
  (132 other events, 1422.7 us)
Sparse Core Ops, SparseCore 0:
  9.5 33.4 all-gather.6
  58.8 19.6 all-gather.8
  80.7 176.0 all-gather.10
  258.2 15.5 all-gather.12
  275.3 30.7 all-gather.14
  307.5 20.7 all-gather.16
  978.8 41.4 all-reduce.11
  1023.4 29.1 reduce-scatter.4
  1055.3 70.6 reduce-scatter.2
where the time goes:
time: 1340 us
  waiting for transfers between devices  821 us (61%)
  blocking collectives  210 us (16%)
  matrix products  103 us (8%)
  local copies, waits for them, and re-layouts  101 us (8%)
  other arithmetic  82.2 us (6%)
  between operations  15.3 us (1%)
    ppermute x16, waiting for transfers between devices, passed_along(): return lax.ppermute(value, axis, pairs)  499 us
    psum x1, blocking collectives, local(): lax.psum((wide_part, out_part, gain_part), 'ctx')  199 us
    all_gather x1, waiting for transfers between devices, local(): key_piece = lax.all_gather(kv_block, 'ctx', axis=1, tiled=True)  170 us
    reduce_scatter x1, waiting for transfers between devices, local(): lax.psum_scatter(jnp.concatenate([jnp.einsum('nd,ne->de', normed_a_low, g...  66 us
    unnamed x10, waiting for transfers between devices  34.8 us
    all_gather x1, waiting for transfers between devices, local(): lax.all_gather(query_key_value_weight, 'shard', axis=0, tiled=True)  32.7 us
    while x192, local copies, waits for them, and re-layouts  28.5 us
    convert_element_type x8, other arithmetic, back_block(): (grad_moving + update).astype(jnp.bfloat16)  28.1 us
  transfers between devices with their start and end apart: 25, of which 21 were waited for; matrix products, arithmetic and copies ran while one was open for 11% of the time, Pallas kernels for 0%

commit v1 on v0

v1 whole, which is shorter than its diff:
```python
import functools

import jax
import jax.numpy as jnp
from jax import lax
from jax.experimental import pallas as pl
from jax.experimental.pallas import tpu as pltpu
from jax.sharding import Mesh, PartitionSpec as P

HEADS = 12
HEAD_DIM = 64
HALF = HEAD_DIM // 2
SCALE = HEAD_DIM ** (-0.5)

epsilon = 1e-05
rope_base = 160000.0
f32 = jnp.float32
bf16 = jnp.bfloat16
VMEM_LIMIT = 56 * 2**20


def low(v):
    return v.astype(bf16)


def swap(v, axis):
    return lax.ppermute(v, axis, [(0, 1), (1, 0)])


def swap_z(v, bit):
    count = lax.axis_size("z")
    return lax.ppermute(v, "z", [(i, i ^ bit) for i in range(count)])


def across(v):
    return lax.ppermute(v, ("x", "core"), [(i, 3 - i) for i in range(4)])


def z_bits():
    bits, bit = [], 1
    while bit < lax.axis_size("z"):
        bits.append(bit)
        bit *= 2
    return bits


def z_offsets():
    offsets = [0]
    for bit in reversed(z_bits()):
        offsets = offsets + [o ^ bit for o in offsets]
    return offsets


SLOT_SHARD = [2 * (e & 1) + (e >> 1) for e in range(4)]


def gather_shard(v):
    from_x = swap(v, "x")
    from_core = swap(v, "core")
    return [v, from_x, from_core, swap(from_x, "core")]


def exchange_shard(parts):
    return [parts[0], swap(parts[1], "x"), swap(parts[2], "core"), across(parts[3])]


def pick(v, index):
    return lax.dynamic_index_in_dim(v, index, 0, keepdims=False)


def pair_in_order(own, other, bit):
    return jnp.where(bit == 0, jnp.stack([own, other]), jnp.stack([other, own]))


def ctx_sum(value, z_index, y_index):
    rest = value.shape[1:]
    value = value.reshape((2, -1) + rest)
    value = pick(value, y_index) + swap(low(pick(value, 1 - y_index)), "y").astype(f32)
    for bit in z_bits():
        mine = (z_index // bit) % 2
        value = value.reshape((2, -1) + rest)
        value = pick(value, mine) + swap_z(low(pick(value, 1 - mine)), bit).astype(f32)
    return value.reshape(rest)


def ctx_gather(value, z_index, y_index):
    rest = value.shape
    value = value[None]
    for bit in reversed(z_bits()):
        value = pair_in_order(value, swap_z(value, bit), (z_index // bit) % 2)
        value = value.reshape((-1,) + rest)
    value = pair_in_order(value, swap(value, "y"), y_index)
    return value.reshape((-1,) + rest)


def norm_parts(values):
    centre = jnp.mean(values, axis=-1, keepdims=True)
    shifted = values - centre
    spread = jnp.mean(shifted * shifted, axis=-1, keepdims=True)
    inv = lax.rsqrt(spread + epsilon)
    return shifted * inv, inv


def norm_back(grad_normed, gain, xhat, inv):
    e = grad_normed * gain
    return inv * (
        e
        - jnp.mean(e, axis=-1, keepdims=True)
        - xhat * jnp.mean(e * xhat, axis=-1, keepdims=True)
    )


def dot(a, b):
    return jnp.dot(a, b, preferred_element_type=f32)


def dot_nt(a, b):
    return lax.dot_general(a, b, (((1,), (1,)), ((), ())), preferred_element_type=f32)


def dot_tn(a, b):
    return lax.dot_general(a, b, (((0,), (0,)), ((), ())), preferred_element_type=f32)


def phi_parts(gate):
    cdf = 0.5 * (1.0 + lax.erf(gate * (0.5**0.5)))
    pdf = jnp.exp(-0.5 * gate * gate) * 0.3989422804014327
    return cdf, pdf


def turn(u, tables, sign):
    cosine, sine_low, sine_high = tables
    turned = pltpu.roll(u, 96, 1) * sine_low + pltpu.roll(u, 32, 1) * sine_high
    return u * cosine + sign * turned


def make_tables(base_cos, base_sin, row_cos, row_sin):
    cosine = base_cos * row_cos - base_sin * row_sin
    sine = base_sin * row_cos + base_cos * row_sin
    is_low = lax.broadcasted_iota(jnp.int32, sine.shape, 1) % HEAD_DIM < HALF
    return cosine, jnp.where(is_low, -sine, 0.0), jnp.where(is_low, 0.0, sine)


def turn_mixed(u, tables, sign):
    is_key = lax.broadcasted_iota(jnp.int32, u.shape, 1) < HEAD_DIM
    return jnp.where(is_key, turn(u, tables, sign), u)


def in_row_order(index_ref, parts, scratch):
    rows = parts[0].shape[0]
    for e, part in enumerate(parts):
        at = pl.multiple_of((index_ref[0] ^ SLOT_SHARD[e]) * rows, rows)
        scratch[pl.ds(at, rows), :] = part[...]


def params():
    return pltpu.CompilerParams(vmem_limit_bytes=VMEM_LIMIT)


IN_SMEM = pl.BlockSpec(memory_space=pltpu.SMEM)
IN_VMEM = pl.BlockSpec(memory_space=pltpu.VMEM)


def prepare_kernel(index_ref, qkv_ref, in_ref, *outs):
    shard = index_ref[0]
    width = qkv_ref.shape[1] // 12
    ff = in_ref.shape[1] // 8
    for s in range(4):

        @pl.when(shard == s)
        def _():
            for e in range(4):
                t = s ^ SLOT_SHARD[e]
                for place, third in enumerate((1, 2, 0)):
                    at = third * 4 * width + t * width
                    outs[e][:, place * width : (place + 1) * width] = qkv_ref[:, at : at + width]
                for half in range(2):
                    at = half * 4 * ff + t * ff
                    outs[4 + e][:, half * ff : (half + 1) * ff] = in_ref[:, at : at + ff]


def prepare(index, w_qkv, w_in):
    rows = w_qkv.shape[0]
    shapes = [jax.ShapeDtypeStruct((rows, w_qkv.shape[1] // 4), bf16)] * 4
    shapes += [jax.ShapeDtypeStruct((rows, w_in.shape[1] // 4), bf16)] * 4
    whole = pl.BlockSpec(memory_space=pltpu.VMEM)
    got = pl.pallas_call(
        prepare_kernel,
        out_shape=shapes,
        in_specs=[pl.BlockSpec(memory_space=pltpu.SMEM), whole, whole],
        out_specs=[whole] * 8,
        compiler_params=pltpu.CompilerParams(vmem_limit_bytes=VMEM_LIMIT),
        name="prepare",
    )(index, w_qkv, w_in)
    return got[:4], got[4:]


def attend_kernel(q_ref, kv_ref, attn_ref, low_ref, lse_ref, max_ref, sum_ref, acc_ref):
    at = pl.program_id(0)
    heads = q_ref.shape[1] // HEAD_DIM
    width = heads * HEAD_DIM

    @pl.when(at == 0)
    def _():
        max_ref[...] = jnp.full(max_ref.shape, -1e30, f32)
        sum_ref[...] = jnp.zeros(sum_ref.shape, f32)
        acc_ref[...] = jnp.zeros(acc_ref.shape, f32)

    block = min(256, q_ref.shape[0])
    for h in range(heads):
        cols = slice(h * HEAD_DIM, (h + 1) * HEAD_DIM)
        key = kv_ref[:, cols]
        value = kv_ref[:, width + h * HEAD_DIM : width + (h + 1) * HEAD_DIM]
        for start in range(0, q_ref.shape[0], block):
            rows = slice(start, start + block)
            scores = dot_nt(q_ref[rows, cols], key)
            old = max_ref[rows, h : h + 1]
            new = jnp.maximum(old, jnp.max(scores, axis=1, keepdims=True))
            weights = jnp.exp(scores - new)
            factor = jnp.exp(old - new)
            max_ref[rows, h : h + 1] = new
            total = sum_ref[rows, h : h + 1] * factor + jnp.sum(weights, axis=1, keepdims=True)
            sum_ref[rows, h : h + 1] = total
            acc = acc_ref[rows, cols] * factor + dot(low(weights), value)
            acc_ref[rows, cols] = acc

    @pl.when(at == pl.num_programs(0) - 1)
    def _():
        for h in range(heads):
            cols = slice(h * HEAD_DIM, (h + 1) * HEAD_DIM)
            attn = acc_ref[:, cols] / sum_ref[:, h : h + 1]
            attn_ref[:, cols] = attn
            low_ref[:, cols] = low(attn)
            lse_ref[:, h : h + 1] = max_ref[:, h : h + 1] + jnp.log(sum_ref[:, h : h + 1])


def attend(query, kv):
    rows, width = query.shape
    chunk = min(2048, kv.shape[0])
    fixed = lambda shape: pl.BlockSpec(shape, lambda i: (0, 0))
    return pl.pallas_call(
        attend_kernel,
        grid=(kv.shape[0] // chunk,),
        in_specs=[fixed((rows, width)), pl.BlockSpec((chunk, 2 * width), lambda i: (i, 0))],
        out_specs=[fixed((rows, width)), fixed((rows, width)), fixed((rows, 128))],
        out_shape=[
            jax.ShapeDtypeStruct((rows, width), f32),
            jax.ShapeDtypeStruct((rows, width), bf16),
            jax.ShapeDtypeStruct((rows, 128), f32),
        ],
        scratch_shapes=[
            pltpu.VMEM((rows, 128), f32),
            pltpu.VMEM((rows, 128), f32),
            pltpu.VMEM((rows, width), f32),
        ],
        compiler_params=pltpu.CompilerParams(vmem_limit_bytes=VMEM_LIMIT),
        name="attend",
    )(query, kv)


def attend_back_kernel(
    q_ref, kv_ref, half_ref, other_ref, w_ref, attn_ref, lse_ref,
    base_cos, base_sin, q_base_cos, q_base_sin, row_cos, row_sin,
    dkv_ref, dq_ref, dq_scr, dkv_scr, lse_scr, delta_scr, grad_scr,
):
    at = pl.program_id(0)
    width = q_ref.shape[1]
    heads = width // HEAD_DIM
    keys = kv_ref.shape[0]
    block = min(512, keys)
    segment = row_cos.shape[0]

    @pl.when(at == 0)
    def _():
        half = half_ref.shape[0]
        grad_scr[:half, :] = low(dot_nt(half_ref[...], w_ref[...]))
        grad_scr[half:, :] = low(dot_nt(other_ref[...], w_ref[...]))
        dq_scr[...] = jnp.zeros(dq_scr.shape, f32)
        lse_scr[...] = lse_ref[...].T
        for h in range(heads):
            cols = slice(h * HEAD_DIM, (h + 1) * HEAD_DIM)
            both = (grad_scr[:, cols].astype(f32) * attn_ref[:, cols]).T
            delta_scr[h : h + 1, :] = jnp.sum(both, axis=0, keepdims=True)

    for h in range(heads):
        cols = slice(h * HEAD_DIM, (h + 1) * HEAD_DIM)
        vcols = slice(width + h * HEAD_DIM, width + (h + 1) * HEAD_DIM)
        query, grad = q_ref[:, cols], grad_scr[:, cols]
        lse, delta = lse_scr[h : h + 1, :], delta_scr[h : h + 1, :]

        def step(i, carry):
            rows = pl.ds(i * block, block)
            key, value = kv_ref[rows, cols], kv_ref[rows, vcols]
            probs = jnp.exp(dot_nt(key, query) - lse)
            dkv_scr[rows, vcols] = dot(low(probs), grad)
            grad_scores = low(probs * (dot_nt(value, grad) - delta))
            dkv_scr[rows, cols] = dot(grad_scores, query)
            dq_scr[cols, :] += dot_tn(key, grad_scores)
            return carry

        lax.fori_loop(0, keys // block, step, 0)

    def finish(i, carry):
        rows = pl.ds(i * segment, segment)
        one = pl.ds(i, 1)
        tables = make_tables(base_cos[one, :], base_sin[one, :], row_cos[...], row_sin[...])
        dkv_ref[rows, :128] = low(turn(dkv_scr[rows, :128], tables, -1.0))
        dkv_ref[rows, 128:256] = low(turn_mixed(dkv_scr[rows, 128:256], tables, -1.0))
        dkv_ref[rows, 256:] = low(dkv_scr[rows, 256:])
        return carry

    lax.fori_loop(0, keys // segment, finish, 0)

    @pl.when(at == pl.num_programs(0) - 1)
    def _():
        first = dq_scr[:128, :].T * SCALE
        second = dq_scr[128:, :].T * SCALE
        for g in range(q_base_cos.shape[0]):
            rows = slice(g * segment, (g + 1) * segment)
            tables = make_tables(
                q_base_cos[g : g + 1, :], q_base_sin[g : g + 1, :], row_cos[...], row_sin[...]
            )
            dq_ref[rows, :128] = low(turn(first[rows], tables, -1.0))
            dq_ref[rows, 128:] = low(turn(second[rows], tables, -1.0)[:, : width - 128])


def attend_back(query, kv, half, other, w_attn, attn, lse, bases, q_bases, row_tables):
    rows, width = query.shape
    chunk = min(2048, kv.shape[0])
    segments = chunk // row_tables[0].shape[0]
    fixed = lambda v: pl.BlockSpec(v.shape, lambda i: (0, 0))
    moving = lambda n, cols: pl.BlockSpec((n, cols), lambda i: (i, 0))
    still = (half, other, w_attn, attn, lse)
    return pl.pallas_call(
        attend_back_kernel,
        grid=(kv.shape[0] // chunk,),
        in_specs=[fixed(query), moving(chunk, 2 * width)]
        + [fixed(v) for v in still]
        + [moving(segments, 128)] * 2
        + [fixed(v) for v in q_bases + row_tables],
        out_specs=[moving(chunk, 2 * width), pl.BlockSpec((rows, width), lambda i: (0, 0))],
        out_shape=[
            jax.ShapeDtypeStruct(kv.shape, bf16),
            jax.ShapeDtypeStruct((rows, width), bf16),
        ],
        scratch_shapes=[
            pltpu.VMEM((256, rows), f32),
            pltpu.VMEM((chunk, 2 * width), f32),
            pltpu.VMEM((128, rows), f32),
            pltpu.VMEM((8, rows), f32),
            pltpu.VMEM((rows, width), bf16),
        ],
        compiler_params=params(),
        name="attend_back",
    )(query, kv, *still, *bases, *q_bases, *row_tables)


def project_kernel(
    index_ref, a_ref, b_ref, base_cos, base_sin, row_cos, row_sin, gain_ref, w0, w1, w2, w3,
    normed_ref, kv_ref, q_ref, w_scr,
):
    width = q_ref.shape[2]
    segment = row_cos.shape[0]

    @pl.when(pl.program_id(0) == 0)
    def _():
        in_row_order(index_ref, (w0, w1, w2, w3), w_scr)

    tokens = a_ref.shape[1]
    block = min(256, tokens)
    w_kv, w_q = w_scr[:, : 2 * width], w_scr[:, 2 * width :]
    for dy, ref in enumerate((a_ref, b_ref)):
        for start in range(0, tokens, block):
            here = slice(start, start + block)
            xhat, _ = norm_parts(ref[0, here, :].astype(f32))
            normed = low(xhat * gain_ref[...])
            normed_ref[0, dy, here, :] = normed
            kv = dot(normed, w_kv)
            for at in range(0, block, segment):
                g = dy * (tokens // segment) + (start + at) // segment
                tables = make_tables(
                    base_cos[0, g : g + 1, :], base_sin[0, g : g + 1, :], row_cos[...], row_sin[...]
                )
                part, into = slice(at, at + segment), slice(start + at, start + at + segment)
                kv_ref[0, dy, into, :128] = low(turn(kv[part, :128], tables, 1.0))
                kv_ref[0, dy, into, 128:256] = low(turn_mixed(kv[part, 128:256], tables, 1.0))
                if start + at == 0:
                    query = dot(normed[part], w_q)
                    query = jnp.concatenate(
                        [query, jnp.zeros((segment, 256 - width), f32)], axis=1
                    )
                    rows = slice(dy * segment, (dy + 1) * segment)
                    q_ref[0, rows, :128] = low(turn(query[:, :128], tables, 1.0) * SCALE)
                    last = low(turn(query[:, 128:], tables, 1.0) * SCALE)
                    q_ref[0, rows, 128:] = last[:, : width - 128]
            kv_ref[0, dy, here, 256:] = low(kv[:, 256:])


def project(index, a_all, b_all, bases, row_tables, gain, weights):
    slots, tokens, features = a_all.shape
    own = row_tables[0].shape[0]
    cols = weights[0].shape[1]
    width = cols // 3
    block = pl.BlockSpec((1, tokens, features), lambda i: (i, 0, 0))
    base = pl.BlockSpec((1,) + bases[0].shape[1:], lambda i: (i, 0, 0))
    wide = lambda n: pl.BlockSpec((1, 2, tokens, n), lambda i: (i, 0, 0, 0))
    return pl.pallas_call(
        project_kernel,
        grid=(slots,),
        in_specs=[IN_SMEM, block, block, base, base] + [IN_VMEM] * 7,
        out_specs=[
            wide(features),
            wide(2 * width),
            pl.BlockSpec((1, 2 * own, width), lambda i: (i, 0, 0)),
        ],
        out_shape=[
            jax.ShapeDtypeStruct((slots, 2, tokens, features), bf16),
            jax.ShapeDtypeStruct((slots, 2, tokens, 2 * width), bf16),
            jax.ShapeDtypeStruct((slots, 2 * own, width), bf16),
        ],
        scratch_shapes=[pltpu.VMEM((features, cols), bf16)],
        compiler_params=params(),
        name="project",
    )(index, a_all, b_all, *bases, *row_tables, gain, *weights)


def middle_kernel(
    index_ref, a_ref, b_ref, t0, t1, t2, t3, wa0, wa1, wa2, wa3, gain_ref,
    wi0, wi1, wi2, wi3, w_out_ref, c0, c1, c2, c3,
    send_ref, keep_ref, send_o_ref, keep_o_ref, mid_ref, normed_ref, hidden_ref, ggu_ref,
    gain_part_ref, w_scr, up_scr,
):
    attn, w_attn, cot = (t0, t1, t2, t3), (wa0, wa1, wa2, wa3), (c0, c1, c2, c3)
    own = a_ref.shape[1]
    tok = 2 * own
    ff = w_out_ref.shape[0]
    in_row_order(index_ref, (wi0, wi1, wi2, wi3), w_scr)
    up_scr[...] = w_scr[:, ff:]
    gain = gain_ref[...]
    gain_part = jnp.zeros(gain.shape, f32)
    for dc in (1, 0):
        rows = slice(dc * 2 * tok, (dc + 1) * 2 * tok)
        mid = jnp.concatenate(
            [r[2 * dc + dx] for dx in range(2) for r in (a_ref, b_ref)]
        ).astype(f32)
        for d in range(4):
            part = [
                attn[d][(d ^ (2 * dc + dx)) * tok : ((d ^ (2 * dc + dx)) + 1) * tok, :]
                for dx in range(2)
            ]
            mid = mid + dot(jnp.concatenate(part), w_attn[d][...])
        xhat, _ = norm_parts(mid)
        normed = low(xhat * gain)
        normed_ref[rows, :] = normed
        w_gate, w_up = w_scr[:, :ff], up_scr[...]
        gate, up = dot(normed, w_gate), dot(normed, w_up)
        cdf, pdf = phi_parts(gate)
        act = gate * cdf
        hidden = low(act * up)
        hidden_ref[rows, :] = hidden
        grad_out = jnp.concatenate([cot[2 * dc][...], cot[2 * dc + 1][...]])
        grad_hidden = dot_nt(grad_out, w_out_ref[...])
        grad_gate = low(grad_hidden * up * (cdf + gate * pdf))
        grad_up = low(grad_hidden * act)
        ggu_ref[rows, :ff] = grad_gate
        ggu_ref[rows, ff:] = grad_up
        part_normed = dot_nt(grad_gate, w_gate) + dot_nt(grad_up, w_up)
        gain_part = gain_part + jnp.sum(part_normed * xhat, axis=0, keepdims=True)
        out_part = dot(hidden, w_out_ref[...])
        if dc:
            send_ref[...] = low(part_normed)
            send_o_ref[...] = low(out_part)
        else:
            keep_ref[...] = part_normed
            keep_o_ref[:tok, :] = out_part[:tok] + mid[:tok]
            keep_o_ref[tok:, :] = out_part[tok:]
            mid_ref[...] = mid
    gain_part_ref[...] = gain_part


def middle_part(index, a_all, b_all, rows, attn, w_attn, gain, w_in, w_out, cot):
    features = gain.shape[1]
    group, ff = attn[0].shape[0], w_out.shape[0]
    half = group // 2
    own = pl.BlockSpec((4, rows, features), lambda i: (0, 0, 0))
    flat = lambda v: pl.BlockSpec(v.shape, lambda i: (0, 0))
    others = [*attn, *w_attn, gain, *w_in, w_out, *cot]
    shapes = [
        ((half, features), bf16), ((half, features), f32),
        ((half, features), bf16), ((half, features), f32),
        ((half, features), f32), ((group, features), bf16),
        ((group, ff), bf16), ((group, 2 * ff), bf16), ((1, features), f32),
    ]
    return pl.pallas_call(
        middle_kernel,
        grid=(1,),
        in_specs=[IN_SMEM, own, own] + [flat(v) for v in others],
        out_specs=[pl.BlockSpec(shape, lambda i: (0, 0)) for shape, _ in shapes],
        out_shape=[jax.ShapeDtypeStruct(*s) for s in shapes],
        scratch_shapes=[pltpu.VMEM((features, 2 * ff), bf16), pltpu.VMEM((features, ff), bf16)],
        compiler_params=params(),
        name="middle_part",
    )(index, a_all, b_all, *others)


def branch_kernel(half_ref, x_ref, mid_ref, c0, c1, gain_ref, branch_ref, grad_ref):
    tok = c0.shape[0]
    for dx, cot in enumerate((c0, c1)):
        rows = slice(dx * tok, (dx + 1) * tok)
        there = slice((1 - dx) * tok, (2 - dx) * tok)
        grad_normed = half_ref[rows, :] + x_ref[there, :].astype(f32)
        xhat, inv = norm_parts(mid_ref[rows, :])
        grad = cot[...].astype(f32) + norm_back(grad_normed, gain_ref[...], xhat, inv)
        branch_ref[rows, :] = low(grad)
        if dx == 0:
            grad_ref[...] = grad


def branch(half_sum, from_x, mid, cot, gain):
    tok, features = cot[0].shape
    return pl.pallas_call(
        branch_kernel,
        in_specs=[IN_VMEM] * 6,
        out_specs=[IN_VMEM] * 2,
        out_shape=[
            jax.ShapeDtypeStruct((2 * tok, features), bf16),
            jax.ShapeDtypeStruct((tok, features), f32),
        ],
        compiler_params=params(),
        name="branch",
    )(half_sum, from_x, mid, cot[0], cot[1], gain)


def tokens_back_kernel(
    index_ref, dkv_ref, dq_ref, a_ref, b_ref, w0, w1, w2, w3, part_ref, gain_ref, w_scr
):
    segment = part_ref.shape[3]
    tokens = a_ref.shape[1]
    width = dq_ref.shape[2]

    @pl.when(pl.program_id(0) == 0)
    def _():
        in_row_order(index_ref, (w0, w1, w2, w3), w_scr)
        gain_ref[...] = jnp.zeros(gain_ref.shape, f32)

    w_kv, w_q = w_scr[:, : 2 * width], w_scr[:, 2 * width :]
    block = min(256, tokens)
    total = jnp.zeros(gain_ref.shape, f32)
    for dy, ref in enumerate((a_ref, b_ref)):
        for start in range(0, tokens, block):
            here = slice(start, start + block)
            part = dot_nt(dkv_ref[0, dy, here, :], w_kv)
            if start == 0:
                own = dot_nt(dq_ref[0, dy * segment : (dy + 1) * segment, :], w_q)
                part = jnp.concatenate([part[:segment] + own, part[segment:]])
            xhat, _ = norm_parts(ref[0, here, :].astype(f32))
            total = total + jnp.sum(part * xhat, axis=0, keepdims=True)
            for at in range(0, block, segment):
                g = (start + at) // segment
                part_ref[0, g, dy, :, :] = part[at : at + segment].astype(part_ref.dtype)
    gain_ref[...] += total


def tokens_back(index, first, d_kv, d_query, a_all, b_all, weights, segment, dtype):
    slots, tokens, features = a_all.shape
    cols = weights[0].shape[1]
    block = pl.BlockSpec((1, tokens, features), lambda i: (i + first, 0, 0))
    count = tokens // segment
    out_block = (1, count, 2, segment, features)
    return pl.pallas_call(
        tokens_back_kernel,
        grid=(2,),
        in_specs=[
            IN_SMEM,
            pl.BlockSpec((1,) + d_kv.shape[1:], lambda i: (i + first, 0, 0, 0)),
            pl.BlockSpec((1,) + d_query.shape[1:], lambda i: (i + first, 0, 0)),
            block,
            block,
        ]
        + [IN_VMEM] * 4,
        out_specs=[
            pl.BlockSpec(out_block, lambda i: (i, 0, 0, 0, 0)),
            pl.BlockSpec((1, features), lambda i: (0, 0)),
        ],
        out_shape=[
            jax.ShapeDtypeStruct((2,) + out_block[1:], dtype),
            jax.ShapeDtypeStruct((1, features), f32),
        ],
        scratch_shapes=[pltpu.VMEM((features, cols), bf16)],
        compiler_params=params(),
        name="tokens_back",
    )(index, d_kv, d_query, a_all, b_all, *weights)


def local(tokens, gain_attn, gain_ffn, w_qkv, w_attn, w_in, w_out, cotangent):
    seq_count, rows, features = tokens.shape
    z_count = lax.axis_size("z")
    x_index, c_index = lax.axis_index("x"), lax.axis_index("core")
    z_index, y_index = lax.axis_index("z"), lax.axis_index("y")
    shard = 2 * x_index + c_index
    shards = 4
    tok = 2 * rows
    group = shards * tok
    width = (HEADS // shards) * HEAD_DIM
    ff = w_out.shape[0]
    w_rows = w_qkv.shape[0]
    slot_of = jnp.take(jnp.array(SLOT_SHARD), jnp.arange(shards) ^ shard)
    index = jnp.stack([shard, y_index]).astype(jnp.int32)

    both = jnp.stack([tokens, cotangent], axis=1)
    mine, theirs = pick(both, y_index), pick(both, 1 - y_index)
    got = swap(theirs, "y")

    def gather_all(piece):
        piece = piece[None]
        for bit in reversed(z_bits()):
            piece = jnp.concatenate([piece, swap_z(piece, bit)])
        piece = jnp.concatenate([piece, swap(piece, "x")])
        piece = jnp.concatenate([piece, swap(piece, "core")])
        return piece.reshape(shards, z_count * rows, features)

    qkv_parts, in_parts = prepare(index, w_qkv, w_in)
    a_all = gather_all(mine[0])
    qkv_parts = exchange_shard(qkv_parts)
    b_all = gather_all(got[0])
    cot = gather_shard(jnp.concatenate([mine[1], got[1]]))
    in_parts = exchange_shard(in_parts)
    attn_parts = gather_shard(w_attn)
    gain_a, gain_f = gain_attn.reshape(1, features), gain_ffn.reshape(1, features)

    z_of = (z_index ^ jnp.array(z_offsets()))[None, None, :]
    s_of = (shard ^ jnp.array(SLOT_SHARD))[:, None, None]
    y_of = (y_index ^ jnp.arange(2))[None, :, None]
    place = ((2 * z_of + y_of) * shards + s_of) * rows
    inverse_freq = jnp.exp(
        (jnp.arange(128) % HALF).astype(f32) * (-1.0 / HALF) * jnp.log(jnp.float32(rope_base))
    )
    base_angles = place[..., None].astype(f32) * inverse_freq
    row_angles = jnp.arange(rows, dtype=f32)[:, None] * inverse_freq
    bases = (jnp.cos(base_angles), jnp.sin(base_angles))
    row_tables = (jnp.cos(row_angles), jnp.sin(row_angles))
    q_bases = tuple(b[:, :, 0].reshape(-1, 128) for b in bases)
    slot_bases = tuple(b.reshape(shards, -1, 128) for b in bases)
    flat_bases = tuple(b.reshape(-1, 128) for b in bases)

    normed_a, kv, query = project(index, a_all, b_all, slot_bases, row_tables, gain_a, qkv_parts)
    query = query.reshape(group, width)
    attn, attn_low, lse = attend(query, kv.reshape(-1, 2 * width))

    got_attn = gather_shard(attn_low)
    send, keep, send_o, keep_o, mid, normed_f, hidden, grad_gate_up, gain_f_part = middle_part(
        index, a_all, b_all, rows, got_attn, attn_parts, gain_f, in_parts, w_out, cot
    )

    half_sum = keep + swap(send, "core").astype(f32)
    half_branch, grad_middle = branch(half_sum, swap(low(half_sum), "x"), mid, cot, gain_f)
    other = swap(half_branch, "core")
    d_kv, d_query = attend_back(
        query, kv.reshape(-1, 2 * width), half_branch, other, w_attn, attn, lse,
        flat_bases, q_bases, row_tables,
    )

    d_kv_slots = d_kv.reshape(kv.shape)
    d_query_slots = d_query.reshape(shards, tok, width)
    back = lambda first, dtype: tokens_back(
        index, first, d_kv_slots, d_query_slots, a_all, b_all, qkv_parts, rows, dtype
    )
    far, gain_far = back(2, bf16)
    near, gain_near = back(0, bf16)
    near = near.astype(f32) + swap(far, "core").astype(f32)
    near = near[0] + swap(low(near[1]), "x").astype(f32)
    for bit in z_bits():
        near = near.reshape((2, -1) + near.shape[1:])
        near = near[0] + swap_z(low(near[1]), bit).astype(f32)
    own = near.reshape(tok, features)
    gain_a_part = gain_far + gain_near

    grad_branch = jnp.concatenate([half_branch, other])
    d_in = dot_tn(normed_f, grad_gate_up)
    d_out = dot_tn(hidden, jnp.concatenate(cot))
    d_attn = dot_tn(attn_low, grad_branch)
    own_normed = normed_a[:, :, :rows].reshape(group, features)
    d_qkv = jnp.concatenate(
        [dot_tn(own_normed, d_query), dot_tn(normed_a.reshape(-1, features), d_kv)], axis=1
    )

    xhat_own, inv_own = norm_parts(jnp.concatenate([a_all[0, :rows], b_all[0, :rows]]).astype(f32))
    grad_tokens = grad_middle + norm_back(own, gain_attn, xhat_own, inv_own)
    out_near = keep_o + swap(send_o, "core").astype(f32)
    out_own = out_near[:tok] + swap(low(out_near[tok:]), "x").astype(f32)
    results = low(jnp.stack([out_own, grad_tokens])).reshape(2, 2, rows, features)
    from_y = swap(results[:, 1], "y")
    output = pair_in_order(results[0, 0], from_y[0], y_index)
    grad_tokens = pair_in_order(results[1, 0], from_y[1], y_index)

    def from_columns(grad, thirds):
        lead = w_rows // (2 * z_count)
        cut = grad.reshape(shards, 2 * z_count, lead, -1).transpose(1, 0, 2, 3)
        total = low(ctx_sum(cut, z_index, y_index))
        parts = exchange_shard([pick(total, shard ^ SLOT_SHARD[e]) for e in range(4)])
        parts = jnp.take(jnp.stack(parts), slot_of, axis=0)
        parts = parts.reshape(shards, lead, thirds, -1).transpose(1, 2, 0, 3).reshape(lead, -1)
        return ctx_gather(parts, z_index, y_index).reshape(w_rows, -1).astype(f32)

    rows_grad = jnp.concatenate([d_out, d_attn])
    rows_grad = jnp.pad(rows_grad, ((0, -rows_grad.shape[0] % (2 * z_count)), (0, 0)))
    rows_grad = rows_grad.reshape(2 * z_count, -1, features)
    rows_grad = ctx_gather(low(ctx_sum(rows_grad, z_index, y_index)), z_index, y_index)
    rows_grad = rows_grad.reshape(-1, features).astype(f32)

    gains = jnp.concatenate([gain_a_part, gain_f_part])
    for axis in ("core", "x", "y"):
        gains = gains + swap(gains, axis)
    for bit in z_bits():
        gains = gains + swap_z(gains, bit)

    return (
        output,
        grad_tokens,
        gains[0],
        gains[1],
        from_columns(d_qkv, 3),
        rows_grad[ff : ff + w_rows],
        from_columns(d_in, 2),
        rows_grad[:ff],
    )


def solution(mesh):
    shards, cycle = mesh.shape["shard"], mesh.shape["ctx"]
    fine = Mesh(mesh.devices.reshape(shards // 2, 2, cycle // 2, 2), ("x", "core", "z", "y"))
    by_token = P(None, ("z", "y", "x", "core"), None)
    by_row = P(("x", "core"), None)
    return jax.shard_map(
        local,
        mesh=fine,
        in_specs=(by_token, P(), P(), by_row, by_row, by_row, by_row, by_token),
        out_specs=(by_token, by_token, P(), P(), by_row, by_row, by_row, by_row),
        check_vma=False,
    )
```

time: 1340 us -> 305 us (0.23)
  waiting for transfers between devices: 821 us -> 130 us
  blocking collectives: 210 us -> 0 us
  matrix products: 103 us -> 7.75 us
  local copies, waits for them, and re-layouts: 101 us -> 27.8 us
  Pallas kernels: 0 us -> 58.3 us
  other arithmetic: 82.2 us -> 26.7 us
  starting transfers between devices: 3.48 us -> 51.6 us
    ppermute x16 -> x63, waiting for transfers between devices: 499 us -> 130 us  [the longest x39 66.9 us: swap(): return lax.ppermute(v, axis, [(0, 1), (1, 0)])]
    all_gather x6 -> x0, waiting for transfers between devices: 222 us -> none  [the longest x1 170 us: local(): key_piece = lax.all_gather(kv_block, 'ctx', axis=1, tiled=True)]
    psum x1 -> x0, blocking collectives: 199 us -> none  [local(): lax.psum((wide_part, out_part, gain_part), 'ctx')]
    dot_general x68 -> x5, matrix products: 103 us -> 7.75 us  [dot_tn(): lax.dot_general(a, b, (((0,), (0,)), ((), ())), preferred_element_type=f32)]
    reduce_scatter x2 -> x0, waiting for transfers between devices: 66 us -> none  [the longest x1 66 us: local(): lax.psum_scatter(jnp.concatenate([jnp.einsum('nd,ne->de', normed_a_low, g...]
    pallas_call x0 -> x8, Pallas kernels: none -> 58.3 us  [the longest x1 18.6 us: attend_back(): pl.pallas_call(attend_back_kernel, grid=(kv.shape[0] // chunk,), in_specs...]
    convert_element_type x24 -> x10, other arithmetic: 58.3 us -> 6.07 us  [the longest x2 2.76 us: from_columns(): return ctx_gather(parts, z_index, y_index).reshape(w_rows, -1).astype(f32)]
    ppermute x16 -> x63, starting transfers between devices: 2.9 us -> 51.6 us  [the longest x39 27.3 us: swap(): return lax.ppermute(v, axis, [(0, 1), (1, 0)])]
  transfers between devices with their start and end apart: 25 -> 63, of which waited for: 21 -> 29; matrix products, arithmetic and copies ran while one was open for 11% -> 16% of each run, Pallas kernels for 0% -> 6%
where the time goes in v1:
time: 305 us; the launch traced here: 304 us
  waiting for transfers between devices  130 us (43%)
  Pallas kernels  58.3 us (19%)
  starting transfers between devices  51.6 us (17%)
  local copies, waits for them, and re-layouts  27.8 us (9%)
  other arithmetic  26.7 us (9%)
  matrix products  7.75 us (3%)
    ppermute x39, waiting for transfers between devices, swap(): return lax.ppermute(v, axis, [(0, 1), (1, 0)])  66.9 us
    ppermute x20, waiting for transfers between devices, swap_z(): return lax.ppermute(v, 'z', [(i, i ^ bit) for i in range(count)])  57.5 us
    ppermute x39, starting transfers between devices, swap(): return lax.ppermute(v, axis, [(0, 1), (1, 0)])  27.3 us
    ppermute x20, starting transfers between devices, swap_z(): return lax.ppermute(v, 'z', [(i, i ^ bit) for i in range(count)])  21.7 us
    pallas_call x1, Pallas kernels, attend_back(): pl.pallas_call(attend_back_kernel, grid=(kv.shape[0] // chunk,), in_specs...  18.6 us
    pallas_call x2, Pallas kernels, tokens_back(): pl.pallas_call(tokens_back_kernel, grid=(2,), in_specs=[IN_SMEM, pl.Block...  8.94 us
    pallas_call x1, Pallas kernels, middle_part(): pl.pallas_call(middle_kernel, grid=(1,), in_specs=[IN_SMEM, own, own] + [...  8.53 us
    pallas_call x1, Pallas kernels, attend(): pl.pallas_call(attend_kernel, grid=(kv.shape[0] // chunk,), in_specs=[fix...  8.47 us
  transfers between devices with their start and end apart: 63, of which 29 were waited for; matrix products, arithmetic and copies ran while one was open for 16% of the time, Pallas kernels for 6%

profile of v1, /device:TPU:0, one launch (start us, length us, event | category | flops | bytes accessed | tf_op | source)
XLA Modules:
  0.0 304.1 jit_solution(10064862583732442709)
XLA Ops:
  0.7 3.0 collective-permute-start.15
  6.4 2.7 collective-permute-start
  16.9 3.3 %prepare.1 = (bf16[192,576]{1,0:T(8,128)(2,1)}, bf16[192,576]{1,0:T(8,128)(2,1)}, bf16[192,576]{1,0:T(8,128)(2,1)}, bf16[192,576]{1,0:T(8,128)(2,1)}, bf16[192,5...) custom-call(s32[2]{0:T(128)} %pad_add_fusion.index_ref, ...), custom_call_target="tpu_custom_call" | custom-call | tf_op jit(solution)/shard_map/prepare/pallas_call | solution.py:187
  22.3 7.0 %collective-permute-done.5 = bf16[1,64,768]{2,1,0:T(8,128)(2,1)S(1)} collective-permute-done((bf16[1,64,768]{2,1,0:T(8,128)(2,1)S(1)}, bf16[1,64,768]{2,1,0:T(8,128)(2,1)S(1)}, u32[]{:S(2)}, u32[]{:S(2)}) %collective-permute-start.5) | collective-permute-done | bytes 98336 | tf_op jit(solution)/shard_map/ppermute | solution.py:32
  31.9 3.2 %collective-permute-done.6 = bf16[2,64,768]{2,1,0:T(8,128)(2,1)S(1)} collective-permute-done((bf16[2,64,768]{2,1,0:T(8,128)(2,1)S(1)}, bf16[2,64,768]{2,1,0:T(8,128)(2,1)S(1)}, u32[]{:S(2)}, u32[]{:S(2)}) %collective-permute-start.6) | collective-permute-done | bytes 196640 | tf_op jit(solution)/shard_map/ppermute | solution.py:32
  35.8 10.2 %collective-permute-done.2 = bf16[4,64,768]{2,1,0:T(8,128)(2,1)S(1)} collective-permute-done((bf16[4,64,768]{2,1,0:T(8,128)(2,1)S(1)}, bf16[4,64,768]{2,1,0:T(8,128)(2,1)S(1)}, u32[]{:S(2)}, u32[]{:S(2)}) %collective-permute-start.2) | collective-permute-done | bytes 393248 | tf_op jit(solution)/shard_map/ppermute | solution.py:27
  46.1 6.1 %collective-permute-done.7 = bf16[4,64,768]{2,1,0:T(8,128)(2,1)S(1)} collective-permute-done((bf16[4,64,768]{2,1,0:T(8,128)(2,1)S(1)}, bf16[4,64,768]{2,1,0:T(8,128)(2,1)S(1)}, u32[]{:S(2)}, u32[]{:S(2)}) %collective-permute-start.7) | collective-permute-done | bytes 393248 | tf_op jit(solution)/shard_map/ppermute | solution.py:27
  53.0 2.8 collective-permute-done.23.c3
  59.4 4.5 %collective-permute-done.11.w3 = bf16[192,576]{1,0:T(8,128)(2,1)S(1)} collective-permute-done((bf16[192,576]{1,0:T(8,128)(2,1)S(1)}, bf16[192,576]{1,0:T(8,128)(2,1)S(1)}, u32[]{:S(2)}, u32[]{:S(2)}) %collective-permute-start.11) | collective-permute-done | bytes 221216 | tf_op jit(solution)/shard_map/ppermute | solution.py:36
  64.8 5.4 %collective-permute-done.9.w1 = bf16[192,576]{1,0:T(8,128)(2,1)S(1)} collective-permute-done((bf16[192,576]{1,0:T(8,128)(2,1)S(1)}, bf16[192,576]{1,0:T(8,128)(2,1)S(1)}, u32[]{:S(2)}, u32[]{:S(2)}) %collective-permute-start.9) | collective-permute-done | bytes 221216 | tf_op jit(solution)/shard_map/ppermute | solution.py:27
  71.0 7.5 %project.1 = (bf16[4,2,256,768]{3,2,1,0:T(8,128)(2,1)}, bf16[4,2,256,384]{3,2,1,0:T(8,128)(2,1)}, bf16[4,128,192]{2,1,0:T(8,128)(2,1)}) custom-call(s32[2]{0:T(128)} %pad_add_fusion.index_ref, bf16[4,256,768]{2,1,0:T(8,128)(2,1)} %bitcast.154, bf16[4,256,768]{2,1,0:T(8,128)(2,1)} %bitcast.159, f32[4,8,128]{2,1,0:T(8,128)} %get-tuple-element.100.base_cos, ...), custom_call_target="tpu_custom_call" | custom-call | tf_op jit(solution)/shard_map/project/pallas_call | solution.py:407
  78.4 8.5 %attend.1 = (f32[512,192]{1,0:T(8,128)}, bf16[512,192]{1,0:T(8,128)(2,1)}, f32[512,128]{1,0:T(8,128)}) custom-call(bf16[512,192]{1,0:T(8,128)(2,1)} %bitcast.187, bf16[2048,384]{1,0:T(8,128)(2,1)} %bitcast.163), custom_call_target="tpu_custom_call" | custom-call | tf_op jit(solution)/shard_map/attend/pallas_call | solution.py:241
  89.6 6.7 %collective-permute-done.12.t1 = bf16[512,192]{1,0:T(8,128)(2,1)S(1)} collective-permute-done((bf16[512,192]{1,0:T(8,128)(2,1)}, bf16[512,192]{1,0:T(8,128)(2,1)S(1)}, u32[]{:S(2)}, u32[]{:S(2)}) %collective-permute-start.12) | collective-permute-done | bytes 196640 | tf_op jit(solution)/shard_map/ppermute | solution.py:27
  100.6 8.5 %middle_part.1 = (bf16[256,768]{1,0:T(8,128)(2,1)}, f32[256,768]{1,0:T(8,128)}, bf16[256,768]{1,0:T(8,128)(2,1)}, f32[256,768]{1,0:T(8,128)}, f32[256,768]{1,0:T...) custom-call(s32[2]{0:T(128)} %pad_add_fusion.index_ref, ...), custom_call_target="tpu_custom_call" | custom-call | tf_op jit(solution)/shard_map/middle_part/pallas_call | solution.py:494
  114.9 10.4 %collective-permute-done.54 = bf16[4,4,24,576]{3,2,0,1:T(8,128)(2,1)S(1)} collective-permute-done((bf16[4,4,24,576]{3,2,0,1:T(8,128)(2,1)S(1)}, bf16[4,4,24,576]{3,2,0,1:T(8,128)(2,1)S(1)}, u32[]{:S(2)}, u32[]{:S(2)}) %collective-permute-start.54) | collective-permute-done | bytes 442400 | tf_op jit(solution)/shard_map/ppermute | solution.py:27
  127.3 5.5 %collective-permute-done.55 = bf16[2,4,24,576]{3,2,1,0:T(8,128)(2,1)S(1)} collective-permute-done((bf16[2,4,24,576]{3,2,1,0:T(8,128)(2,1)S(1)}, bf16[2,4,24,576]{3,2,1,0:T(8,128)(2,1)S(1)}, u32[]{:S(2)}, u32[]{:S(2)}) %collective-permute-start.55) | collective-permute-done | bytes 221216 | tf_op jit(solution)/shard_map/ppermute | solution.py:32
  135.5 4.6 %collective-permute-done.56 = bf16[1,4,24,576]{3,2,1,0:T(8,128)(2,1)S(1)} collective-permute-done((bf16[1,4,24,576]{3,2,1,0:T(8,128)(2,1)S(1)}, bf16[1,4,24,576]{3,2,1,0:T(8,128)(2,1)S(1)}, u32[]{:S(2)}, u32[]{:S(2)}) %collective-permute-start.56) | collective-permute-done | bytes 110624 | tf_op jit(solution)/shard_map/ppermute | solution.py:32
  140.9 3.0 %branch.1 = (bf16[256,768]{1,0:T(8,128)(2,1)}, f32[128,768]{1,0:T(8,128)}) custom-call(f32[256,768]{1,0:T(8,128)} %get-tuple-element.79.half_ref, bf16[256,768]{1,0:T(8,128)(2,1)} %copy-done.26, f32[256,768]{1,0:T(8,128)} %get-tuple-element.55.mid_ref, bf16[128,768]{1,0:T(8,128)(2,1)} %copy-done.8, bf16[128,768]{1,0:T(8,128)(2,1)} %copy-done.9, ...), custom_call_target="tpu_custom_call" | custom-call | tf_op jit(solution)/shard_map/branch/pallas_call | solution.py:521
  150.3 18.6 %attend_back.1 = (bf16[2048,384]{1,0:T(8,128)(2,1)}, bf16[512,192]{1,0:T(8,128)(2,1)}) custom-call(bf16[512,192]{1,0:T(8,128)(2,1)} %bitcast.188, bf16[2048,384]{1,0:T(8,128)(2,1)} %bitcast.164, bf16[256,768]{1,0:T(8,128)(2,1)} %get-tuple-element.57.half_ref, bf16[256,768]{1,0:T(8,128)(2,1)} %copy-done.24, bf16[192,768]{1,0:T(8,128)(2,1)} %w_ref.1, ...), custom_call_target="tpu_custom_call" | custom-call | tf_op jit(solution)/shard_map/attend_back/pallas_call | solution.py:334
  173.6 4.4 %tokens_back.2 = (bf16[2,4,2,64,768]{4,3,2,1,0:T(8,128)(2,1)}, f32[1,768]{1,0:T(1,128)}) custom-call(s32[2]{0:T(128)} %pad_add_fusion.index_ref, bf16[4,2,256,384]{3,2,1,0:T(8,128)(2,1)} %bitcast.165, bf16[4,128,192]{2,1,0:T(8,128)(2,1)} %bitcast.178, bf16[4,256,768]{2,1,0:T(8,128)(2,1)} %bitcast.156, bf16[4,256,768]{2,1,0:T(8,128)(2,1)} %bitcast.161, ...), custom_call_target="tpu_custom_call" | custom-call | tf_op jit(solution)/shard_map/tokens_back/pallas_call | solution.py:570
  178.1 4.5 %tokens_back.3 = (bf16[2,4,2,64,768]{4,3,2,1,0:T(8,128)(2,1)}, f32[1,768]{1,0:T(1,128)}) custom-call(s32[2]{0:T(128)} %pad_add_fusion.index_ref, bf16[4,2,256,384]{3,2,1,0:T(8,128)(2,1)} %bitcast.166, bf16[4,128,192]{2,1,0:T(8,128)(2,1)} %bitcast.179, bf16[4,256,768]{2,1,0:T(8,128)(2,1)} %bitcast.157, bf16[4,256,768]{2,1,0:T(8,128)(2,1)} %bitcast.162, ...), custom_call_target="tpu_custom_call" | custom-call | tf_op jit(solution)/shard_map/tokens_back/pallas_call | solution.py:570
  196.6 3.4 %collective-permute-start.38 = (f32[2,768]{1,0:T(2,128)S(1)}, f32[2,768]{1,0:T(2,128)S(1)}, u32[]{:S(2)}, u32[]{:S(2)}) collective-permute-start(f32[2,768]{1,0:T(2,128)S(1)} %add.280), channel_id=1, source_target_pairs={{0,4},{2,6},{4,0},{6,2},{1,5},{3,7},{5,1},{7,3},{8,12},{10,14},{12... | collective-permute-start | bytes 18440 | tf_op jit(solution)/shard_map/ppermute | solution.py:32
  204.4 7.4 %collective-permute-done.39 = bf16[4,4,24,576]{3,2,0,1:T(8,128)(2,1)S(1)} collective-permute-done((bf16[4,4,24,576]{3,2,0,1:T(8,128)(2,1)S(1)}, bf16[4,4,24,576]{3,2,0,1:T(8,128)(2,1)S(1)}, u32[]{:S(2)}, u32[]{:S(2)}) %collective-permute-start.39) | collective-permute-done | bytes 442400 | tf_op jit(solution)/shard_map/ppermute | solution.py:27
  214.6 5.7 %collective-permute-done.40 = bf16[2,4,24,576]{3,2,1,0:T(8,128)(2,1)S(1)} collective-permute-done((bf16[2,4,24,576]{3,2,1,0:T(8,128)(2,1)S(1)}, bf16[2,4,24,576]{3,2,1,0:T(8,128)(2,1)S(1)}, u32[]{:S(2)}, u32[]{:S(2)}) %collective-permute-start.40) | collective-permute-done | bytes 221216 | tf_op jit(solution)/shard_map/ppermute | solution.py:32
  223.4 4.2 %collective-permute-done.41 = bf16[1,4,24,576]{3,2,1,0:T(8,128)(2,1)S(1)} collective-permute-done((bf16[1,4,24,576]{3,2,1,0:T(8,128)(2,1)S(1)}, bf16[1,4,24,576]{3,2,1,0:T(8,128)(2,1)S(1)}, u32[]{:S(2)}, u32[]{:S(2)}) %collective-permute-start.41) | collective-permute-done | bytes 110624 | tf_op jit(solution)/shard_map/ppermute | solution.py:32
  234.5 3.0 collective-permute-start.45
  237.5 7.2 %collective-permute-done.60 = bf16[1,24,2304]{2,1,0:T(8,128)(2,1)S(1)} collective-permute-done((bf16[1,24,2304]{2,1,0:T(8,128)(2,1)S(1)}, bf16[1,24,2304]{2,1,0:T(8,128)(2,1)S(1)}, u32[]{:S(2)}, u32[]{:S(2)}) %collective-permute-start.60) | collective-permute-done | bytes 110624 | tf_op jit(solution)/shard_map/ppermute | solution.py:32
  249.0 4.1 %collective-permute-done.61 = bf16[2,24,2304]{2,1,0:T(8,128)(2,1)S(1)} collective-permute-done((bf16[2,24,2304]{2,1,0:T(8,128)(2,1)S(1)}, bf16[2,24,2304]{2,1,0:T(8,128)(2,1)S(1)}, u32[]{:S(2)}, u32[]{:S(2)}) %collective-permute-start.61) | collective-permute-done | bytes 221216 | tf_op jit(solution)/shard_map/ppermute | solution.py:32
  271.2 5.7 %collective-permute-done.30 = bf16[4,2,64,768]{3,2,1,0:T(8,128)(2,1)} collective-permute-done((bf16[4,2,64,768]{3,2,1,0:T(8,128)(2,1)}, bf16[4,2,64,768]{3,2,1,0:T(8,128)(2,1)}, u32[]{:S(2)}, u32[]{:S(2)}) %collective-permute-start.30) | collective-permute-done | bytes 786464 | tf_op jit(solution)/shard_map/ppermute | solution.py:27
  281.8 5.6 %collective-permute-done.31 = bf16[2,2,64,768]{3,2,1,0:T(8,128)(2,1)S(1)} collective-permute-done((bf16[2,2,64,768]{3,2,1,0:T(8,128)(2,1)S(1)}, bf16[2,2,64,768]{3,2,1,0:T(8,128)(2,1)S(1)}, u32[]{:S(2)}, u32[]{:S(2)}) %collective-permute-start.31) | collective-permute-done | bytes 393248 | tf_op jit(solution)/shard_map/ppermute | solution.py:32
  289.0 7.3 %collective-permute-done.32 = bf16[1,2,64,768]{3,2,1,0:T(8,128)(2,1)S(1)} collective-permute-done((bf16[1,2,64,768]{3,2,1,0:T(8,128)(2,1)S(1)}, bf16[1,2,64,768]{3,2,1,0:T(8,128)(2,1)S(1)}, u32[]{:S(2)}, u32[]{:S(2)}) %collective-permute-start.32) | collective-permute-done | bytes 196640 | tf_op jit(solution)/shard_map/ppermute | solution.py:32
  297.0 5.6 %collective-permute-done.33 = bf16[2,64,768]{2,1,0:T(8,128)(2,1)S(1)} collective-permute-done((bf16[2,64,768]{2,1,0:T(8,128)(2,1)S(1)}, bf16[2,64,768]{2,1,0:T(8,128)(2,1)S(1)}, u32[]{:S(2)}, u32[]{:S(2)}) %collective-permute-start.33) | collective-permute-done | bytes 196640 | tf_op jit(solution)/shard_map/ppermute | solution.py:27
  (363 shorter events, 112.6 us)
Async XLA Ops:
  0.7 87.2 %collective-permute-start.15 = (bf16[192,768]{1,0:T(8,128)(2,1)}, bf16[192,768]{1,0:T(8,128)(2,1)S(1)}, u32[]{:S(2)}, u32[]{:S(2)}) collective-permute-start(bf16[192,768]{1,0:T(8,128)(2,1)} %w_ref.1), channel_id=1, source_target_pairs={{0,16},{16,0},{1,17},{17,1},{2,18},{18,2},{3,19},{19,3},{4,20},{20... | collective-permute-start | bytes 884744 | tf_op jit(solution)/shard_map/ppermute | solution.py:27
  3.7 95.9 %collective-permute-start.16 = (bf16[192,768]{1,0:T(8,128)(2,1)}, bf16[192,768]{1,0:T(8,128)(2,1)}, u32[]{:S(2)}, u32[]{:S(2)}) collective-permute-start(bf16[192,768]{1,0:T(8,128)(2,1)} %w_ref.1), channel_id=1, source_target_pairs={{0,8},{8,0},{1,9},{9,1},{2,10},{10,2},{3,11},{11,3},{4,12},{12,4},... | collective-permute-start | bytes 884744 | tf_op jit(solution)/shard_map/ppermute | solution.py:27
  4.8 17.1 %collective-permute-start.4 = (bf16[2,64,768]{2,1,0:T(8,128)(2,1)S(1)}, bf16[2,64,768]{2,1,0:T(8,128)(2,1)S(1)}, u32[]{:S(2)}, u32[]{:S(2)}) collective-permute-start(bf16[2,64,768]{2,1,0:T(8,128)(2,1)S(1)} %get-tuple-element.80), channel_id=1, source_target_pairs={{0,1},{1,0},{2,3},{3,2},{4,5},{5,4},{6,7},{7,6},{8,9},{9,8},{10,11... | collective-permute-start | bytes 589832 | tf_op jit(solution)/shard_map/ppermute | solution.py:27
  6.4 13.8 %collective-permute-start = (bf16[1,64,768]{2,1,0:T(8,128)(2,1)S(1)}, bf16[1,64,768]{2,1,0:T(8,128)(2,1)S(1)}, u32[]{:S(2)}, u32[]{:S(2)}) collective-permute-start(bf16[1,64,768]{2,1,0:T(8,128)(2,1)S(1)} %get-tuple-element.85), channel_id=1, source_target_pairs={{0,4},{2,6},{4,0},{6,2},{1,5},{3,7},{5,1},{7,3},{8,12},{10,14},{12... | collective-permute-start | bytes 294920 | tf_op jit(solution)/shard_map/ppermute | solution.py:32
  20.2 10.1 %collective-permute-start.1 = (bf16[2,64,768]{2,1,0:T(8,128)(2,1)S(1)}, bf16[2,64,768]{2,1,0:T(8,128)(2,1)S(1)}, u32[]{:S(2)}, u32[]{:S(2)}) collective-permute-start(bf16[2,64,768]{2,1,0:T(8,128)(2,1)S(1)} %pad_maximum_fusion.7), channel_id=1, source_target_pairs={{0,2},{2,0},{4,6},{6,4},{1,3},{3,1},{5,7},{7,5},{8,10},{10,8},{12,... | collective-permute-start | bytes 589832 | tf_op jit(solution)/shard_map/ppermute | solution.py:32
  29.7 22.5 %collective-permute-start.21 = (bf16[128,768]{1,0:T(8,128)(2,1)S(1)}, bf16[128,768]{1,0:T(8,128)(2,1)S(1)}, u32[]{:S(2)}, u32[]{:S(2)}) collective-permute-start(bf16[128,768]{1,0:T(8,128)(2,1)S(1)} %pad_maximum_fusion.9.c0), channel_id=1, source_target_pairs={{0,16},{16,0},{1,17},{17,1},{2,18},{18,2},{3,19},{19,3},{4,20},{20... | collective-permute-start | bytes 589832 | tf_op jit(solution)/shard_map/ppermute | solution.py:27
  30.3 15.6 %collective-permute-start.2 = (bf16[4,64,768]{2,1,0:T(8,128)(2,1)S(1)}, bf16[4,64,768]{2,1,0:T(8,128)(2,1)S(1)}, u32[]{:S(2)}, u32[]{:S(2)}) collective-permute-start(bf16[4,64,768]{2,1,0:T(8,128)(2,1)S(1)} %pad_maximum_fusion.4), channel_id=1, source_target_pairs={{0,16},{16,0},{1,17},{17,1},{2,18},{18,2},{3,19},{19,3},{4,20},{20... | collective-permute-start | bytes 1179656 | tf_op jit(solution)/shard_map/ppermute | solution.py:27
  35.1 17.0 %collective-permute-start.7 = (bf16[4,64,768]{2,1,0:T(8,128)(2,1)S(1)}, bf16[4,64,768]{2,1,0:T(8,128)(2,1)S(1)}, u32[]{:S(2)}, u32[]{:S(2)}) collective-permute-start(bf16[4,64,768]{2,1,0:T(8,128)(2,1)S(1)} %pad_maximum_fusion.5), channel_id=1, source_target_pairs={{0,16},{16,0},{1,17},{17,1},{2,18},{18,2},{3,19},{19,3},{4,20},{20... | collective-permute-start | bytes 1179656 | tf_op jit(solution)/shard_map/ppermute | solution.py:27
  57.2 13.0 %collective-permute-start.9 = (bf16[192,576]{1,0:T(8,128)(2,1)S(1)}, bf16[192,576]{1,0:T(8,128)(2,1)S(1)}, u32[]{:S(2)}, u32[]{:S(2)}) collective-permute-start(bf16[192,576]{1,0:T(8,128)(2,1)S(1)} %copy-done.55), channel_id=1, source_target_pairs={{0,16},{16,0},{1,17},{17,1},{2,18},{18,2},{3,19},{19,3},{4,20},{20... | collective-permute-start | bytes 663560 | tf_op jit(solution)/shard_map/ppermute | solution.py:27
  58.5 29.3 %collective-permute-start.18 = (bf16[192,576]{1,0:T(8,128)(2,1)S(1)}, bf16[192,576]{1,0:T(8,128)(2,1)S(1)}, u32[]{:S(2)}, u32[]{:S(2)}) collective-permute-start(bf16[192,576]{1,0:T(8,128)(2,1)S(1)} %copy-done.54), channel_id=1, source_target_pairs={{0,16},{16,0},{1,17},{17,1},{2,18},{18,2},{3,19},{19,3},{4,20},{20... | collective-permute-start | bytes 663560 | tf_op jit(solution)/shard_map/ppermute | solution.py:27
  63.9 25.6 %collective-permute-start.19 = (bf16[192,576]{1,0:T(8,128)(2,1)S(1)}, bf16[192,576]{1,0:T(8,128)(2,1)S(1)}, u32[]{:S(2)}, u32[]{:S(2)}) collective-permute-start(bf16[192,576]{1,0:T(8,128)(2,1)S(1)} %copy-done.53), channel_id=1, source_target_pairs={{0,8},{8,0},{1,9},{9,1},{2,10},{10,2},{3,11},{11,3},{4,12},{12,4},... | collective-permute-start | bytes 663560 | tf_op jit(solution)/shard_map/ppermute | solution.py:27
  86.9 9.4 %collective-permute-start.12 = (bf16[512,192]{1,0:T(8,128)(2,1)}, bf16[512,192]{1,0:T(8,128)(2,1)S(1)}, u32[]{:S(2)}, u32[]{:S(2)}) collective-permute-start(bf16[512,192]{1,0:T(8,128)(2,1)} %get-tuple-element.46.t0), channel_id=1, source_target_pairs={{0,16},{16,0},{1,17},{17,1},{2,18},{18,2},{3,19},{19,3},{4,20},{20... | collective-permute-start | bytes 589832 | tf_op jit(solution)/shard_map/ppermute | solution.py:27
  87.8 11.8 %collective-permute-start.20 = (bf16[192,576]{1,0:T(8,128)(2,1)S(1)}, bf16[192,576]{1,0:T(8,128)(2,1)S(1)}, u32[]{:S(2)}, u32[]{:S(2)}) collective-permute-start(bf16[192,576]{1,0:T(8,128)(2,1)S(1)} %copy-done.52), channel_id=1, source_target_pairs={{0,24},{8,16},{16,8},{24,0},{1,25},{9,17},{17,9},{25,1},{2,26},{10... | collective-permute-start | bytes 663560 | tf_op jit(solution)/shard_map/ppermute | solution.py:36
  87.9 11.7 %collective-permute-start.17 = (bf16[192,768]{1,0:T(8,128)(2,1)S(1)}, bf16[192,768]{1,0:T(8,128)(2,1)S(1)}, u32[]{:S(2)}, u32[]{:S(2)}) collective-permute-start(bf16[192,768]{1,0:T(8,128)(2,1)S(1)} %collective-permute-done.15.wa1), channel_id=1, source_target_pairs={{0,8},{8,0},{1,9},{9,1},{2,10},{10,2},{3,11},{11,3},{4,12},{12,4},... | collective-permute-start | bytes 884744 | tf_op jit(solution)/shard_map/ppermute | solution.py:27
  89.5 10.1 %collective-permute-start.13 = (bf16[512,192]{1,0:T(8,128)(2,1)}, bf16[512,192]{1,0:T(8,128)(2,1)S(1)}, u32[]{:S(2)}, u32[]{:S(2)}) collective-permute-start(bf16[512,192]{1,0:T(8,128)(2,1)} %get-tuple-element.46.t0), channel_id=1, source_target_pairs={{0,8},{8,0},{1,9},{9,1},{2,10},{10,2},{3,11},{11,3},{4,12},{12,4},... | collective-permute-start | bytes 589832 | tf_op jit(solution)/shard_map/ppermute | solution.py:27
  112.1 13.2 %collective-permute-start.54 = (bf16[4,4,24,576]{3,2,0,1:T(8,128)(2,1)S(1)}, bf16[4,4,24,576]{3,2,0,1:T(8,128)(2,1)S(1)}, u32[]{:S(2)}, u32[]{:S(2)}) collective-permute-start(bf16[4,4,24,576]{3,2,0,1:T(8,128)(2,1)S(1)} %fusion.8), channel_id=1, source_target_pairs={{0,1},{1,0},{2,3},{3,2},{4,5},{5,4},{6,7},{7,6},{8,9},{9,8},{10,11... | collective-permute-start | bytes 1327112 | tf_op jit(solution)/shard_map/ppermute | solution.py:27
  112.7 13.9 %collective-permute-start.24 = (bf16[256,768]{1,0:T(8,128)(2,1)S(1)}, bf16[256,768]{1,0:T(8,128)(2,1)S(1)}, u32[]{:S(2)}, u32[]{:S(2)}) collective-permute-start(bf16[256,768]{1,0:T(8,128)(2,1)S(1)} %copy-done.51), channel_id=1, source_target_pairs={{0,8},{8,0},{1,9},{9,1},{2,10},{10,2},{3,11},{11,3},{4,12},{12,4},... | collective-permute-start | bytes 1179656 | tf_op jit(solution)/shard_map/ppermute | solution.py:27
  114.1 26.0 %collective-permute-start.27 = (bf16[256,768]{1,0:T(8,128)(2,1)S(1)}, bf16[256,768]{1,0:T(8,128)(2,1)S(1)}, u32[]{:S(2)}, u32[]{:S(2)}) collective-permute-start(bf16[256,768]{1,0:T(8,128)(2,1)S(1)} %get-tuple-element.78), channel_id=1, source_target_pairs={{0,16},{16,0},{1,17},{17,1},{2,18},{18,2},{3,19},{19,3},{4,20},{20... | collective-permute-start | bytes 1179656 | tf_op jit(solution)/shard_map/ppermute | solution.py:27
  189.8 12.8 %collective-permute-start.48 = (bf16[4,60,768]{2,1,0:T(8,128)(2,1)}, bf16[4,60,768]{2,1,0:T(8,128)(2,1)}, u32[]{:S(2)}, u32[]{:S(2)}) collective-permute-start(bf16[4,60,768]{2,1,0:T(8,128)(2,1)} %fusion.9), channel_id=1, source_target_pairs={{0,1},{1,0},{2,3},{3,2},{4,5},{5,4},{6,7},{7,6},{8,9},{9,8},{10,11... | collective-permute-start | bytes 1105928 | tf_op jit(solution)/shard_map/ppermute | solution.py:27
  201.4 10.4 %collective-permute-start.39 = (bf16[4,4,24,576]{3,2,0,1:T(8,128)(2,1)S(1)}, bf16[4,4,24,576]{3,2,0,1:T(8,128)(2,1)S(1)}, u32[]{:S(2)}, u32[]{:S(2)}) collective-permute-start(bf16[4,4,24,576]{3,2,0,1:T(8,128)(2,1)S(1)} %fusion.7), channel_id=1, source_target_pairs={{0,1},{1,0},{2,3},{3,2},{4,5},{5,4},{6,7},{7,6},{8,9},{9,8},{10,11... | collective-permute-start | bytes 1327112 | tf_op jit(solution)/shard_map/ppermute | solution.py:27
  201.9 53.8 %collective-permute-start.29 = (bf16[2,4,2,64,768]{4,3,2,1,0:T(8,128)(2,1)}, bf16[2,4,2,64,768]{4,3,2,1,0:T(8,128)(2,1)S(1)}, u32[]{:S(2)}, u32[]{:S(2)}) collective-permute-start(bf16[2,4,2,64,768]{4,3,2,1,0:T(8,128)(2,1)} %get-tuple-element.63), channel_id=1, source_target_pairs={{0,8},{8,0},{1,9},{9,1},{2,10},{10,2},{3,11},{11,3},{4,12},{12,4},... | collective-permute-start | bytes 4718600 | tf_op jit(solution)/shard_map/ppermute | solution.py:27
  203.6 8.8 %collective-permute-start.49 = (bf16[2,60,768]{2,1,0:T(8,128)(2,1)S(1)}, bf16[2,60,768]{2,1,0:T(8,128)(2,1)S(1)}, u32[]{:S(2)}, u32[]{:S(2)}) collective-permute-start(bf16[2,60,768]{2,1,0:T(8,128)(2,1)S(1)} %fusion.18), channel_id=1, source_target_pairs={{0,2},{2,0},{4,6},{6,4},{1,3},{3,1},{5,7},{7,5},{8,10},{10,8},{12,... | collective-permute-start | bytes 552968 | tf_op jit(solution)/shard_map/ppermute | solution.py:32
  212.5 8.8 %collective-permute-start.50 = (bf16[1,60,768]{2,1,0:T(8,128)(2,1)S(1)}, bf16[1,60,768]{2,1,0:T(8,128)(2,1)S(1)}, u32[]{:S(2)}, u32[]{:S(2)}) collective-permute-start(bf16[1,60,768]{2,1,0:T(8,128)(2,1)S(1)} %dynamic-slice_convert_fusion.8), channel_id=1, source_target_pairs={{0,4},{2,6},{4,0},{6,2},{1,5},{3,7},{5,1},{7,3},{8,12},{10,14},{12... | collective-permute-start | bytes 276488 | tf_op jit(solution)/shard_map/ppermute | solution.py:32
  229.9 17.3 %collective-permute-start.52 = (bf16[2,60,768]{2,1,0:T(8,128)(2,1)S(1)}, bf16[2,60,768]{2,1,0:T(8,128)(2,1)S(1)}, u32[]{:S(2)}, u32[]{:S(2)}) collective-permute-start(bf16[2,60,768]{2,1,0:T(8,128)(2,1)S(1)} %maximum_select_fusion.13), channel_id=1, source_target_pairs={{0,2},{2,0},{4,6},{6,4},{1,3},{3,1},{5,7},{7,5},{8,10},{10,8},{12,... | collective-permute-start | bytes 552968 | tf_op jit(solution)/shard_map/ppermute | solution.py:32
  233.6 11.0 %collective-permute-start.60 = (bf16[1,24,2304]{2,1,0:T(8,128)(2,1)S(1)}, bf16[1,24,2304]{2,1,0:T(8,128)(2,1)S(1)}, u32[]{:S(2)}, u32[]{:S(2)}) collective-permute-start(bf16[1,24,2304]{2,1,0:T(8,128)(2,1)S(1)} %broadcast_in_dim_reshape.7), channel_id=1, source_target_pairs={{0,4},{2,6},{4,0},{6,2},{1,5},{3,7},{5,1},{7,3},{8,12},{10,14},{12... | collective-permute-start | bytes 331784 | tf_op jit(solution)/shard_map/ppermute | solution.py:32
  234.5 12.5 %collective-permute-start.45 = (bf16[1,24,2304]{2,1,0:T(8,128)(2,1)S(1)}, bf16[1,24,2304]{2,1,0:T(8,128)(2,1)S(1)}, u32[]{:S(2)}, u32[]{:S(2)}) collective-permute-start(bf16[1,24,2304]{2,1,0:T(8,128)(2,1)S(1)} %broadcast_in_dim_reshape.6), channel_id=1, source_target_pairs={{0,4},{2,6},{4,0},{6,2},{1,5},{3,7},{5,1},{7,3},{8,12},{10,14},{12... | collective-permute-start | bytes 331784 | tf_op jit(solution)/shard_map/ppermute | solution.py:32
  247.0 13.4 %collective-permute-start.46 = (bf16[2,24,2304]{2,1,0:T(8,128)(2,1)S(1)}, bf16[2,24,2304]{2,1,0:T(8,128)(2,1)S(1)}, u32[]{:S(2)}, u32[]{:S(2)}) collective-permute-start(bf16[2,24,2304]{2,1,0:T(8,128)(2,1)S(1)} %maximum_select_fusion.7), channel_id=1, source_target_pairs={{0,2},{2,0},{4,6},{6,4},{1,3},{3,1},{5,7},{7,5},{8,10},{10,8},{12,... | collective-permute-start | bytes 663560 | tf_op jit(solution)/shard_map/ppermute | solution.py:32
  247.2 14.5 %collective-permute-start.53 = (bf16[4,60,768]{2,1,0:T(8,128)(2,1)S(1)}, bf16[4,60,768]{2,1,0:T(8,128)(2,1)S(1)}, u32[]{:S(2)}, u32[]{:S(2)}) collective-permute-start(bf16[4,60,768]{2,1,0:T(8,128)(2,1)S(1)} %bitcast.180), channel_id=1, source_target_pairs={{0,1},{1,0},{2,3},{3,2},{4,5},{5,4},{6,7},{7,6},{8,9},{9,8},{10,11... | collective-permute-start | bytes 1105928 | tf_op jit(solution)/shard_map/ppermute | solution.py:27
  253.9 15.7 %collective-permute-start.62 = (bf16[4,24,2304]{2,1,0:T(8,128)(2,1)}, bf16[4,24,2304]{2,1,0:T(8,128)(2,1)}, u32[]{:S(2)}, u32[]{:S(2)}) collective-permute-start(bf16[4,24,2304]{2,1,0:T(8,128)(2,1)} %bitcast.86), channel_id=1, source_target_pairs={{0,1},{1,0},{2,3},{3,2},{4,5},{5,4},{6,7},{7,6},{8,9},{9,8},{10,11... | collective-permute-start | bytes 1327112 | tf_op jit(solution)/shard_map/ppermute | solution.py:27
  259.6 17.2 %collective-permute-start.30 = (bf16[4,2,64,768]{3,2,1,0:T(8,128)(2,1)}, bf16[4,2,64,768]{3,2,1,0:T(8,128)(2,1)}, u32[]{:S(2)}, u32[]{:S(2)}) collective-permute-start(bf16[4,2,64,768]{3,2,1,0:T(8,128)(2,1)} %fusion.1), channel_id=1, source_target_pairs={{0,16},{16,0},{1,17},{17,1},{2,18},{18,2},{3,19},{19,3},{4,20},{20... | collective-permute-start | bytes 2359304 | tf_op jit(solution)/shard_map/ppermute | solution.py:27
  261.3 18.9 %collective-permute-start.47 = (bf16[4,24,2304]{2,1,0:T(8,128)(2,1)}, bf16[4,24,2304]{2,1,0:T(8,128)(2,1)}, u32[]{:S(2)}, u32[]{:S(2)}) collective-permute-start(bf16[4,24,2304]{2,1,0:T(8,128)(2,1)} %bitcast.51), channel_id=1, source_target_pairs={{0,1},{1,0},{2,3},{3,2},{4,5},{5,4},{6,7},{7,6},{8,9},{9,8},{10,11... | collective-permute-start | bytes 1327112 | tf_op jit(solution)/shard_map/ppermute | solution.py:27
  278.2 9.2 %collective-permute-start.31 = (bf16[2,2,64,768]{3,2,1,0:T(8,128)(2,1)S(1)}, bf16[2,2,64,768]{3,2,1,0:T(8,128)(2,1)S(1)}, u32[]{:S(2)}, u32[]{:S(2)}) collective-permute-start(bf16[2,2,64,768]{3,2,1,0:T(8,128)(2,1)S(1)} %slice.181), channel_id=1, source_target_pairs={{0,2},{2,0},{4,6},{6,4},{1,3},{3,1},{5,7},{7,5},{8,10},{10,8},{12,... | collective-permute-start | bytes 1179656 | tf_op jit(solution)/shard_map/ppermute | solution.py:32
  (89 other events, 605.4 us)

commit v2 on v1

--- a/solution.py
+++ b/solution.py
@@ -64,6 +64,10 @@
     return [parts[0], swap(parts[1], "x"), swap(parts[2], "core"), across(parts[3])]
 
 
+def after(value, *others):
+    return lax.optimization_barrier((value, others))[0]
+
+
 def pick(v, index):
     return lax.dynamic_index_in_dim(v, index, 0, keepdims=False)
 
@@ -72,25 +76,21 @@
     return jnp.where(bit == 0, jnp.stack([own, other]), jnp.stack([other, own]))
 
 
-def ctx_sum(value, z_index, y_index):
-    rest = value.shape[1:]
-    value = value.reshape((2, -1) + rest)
-    value = pick(value, y_index) + swap(low(pick(value, 1 - y_index)), "y").astype(f32)
-    for bit in z_bits():
-        mine = (z_index // bit) % 2
-        value = value.reshape((2, -1) + rest)
-        value = pick(value, mine) + swap_z(low(pick(value, 1 - mine)), bit).astype(f32)
-    return value.reshape(rest)
-
-
-def ctx_gather(value, z_index, y_index):
-    rest = value.shape
-    value = value[None]
-    for bit in reversed(z_bits()):
-        value = pair_in_order(value, swap_z(value, bit), (z_index // bit) % 2)
-        value = value.reshape((-1,) + rest)
-    value = pair_in_order(value, swap(value, "y"), y_index)
-    return value.reshape((-1,) + rest)
+def first_half(value, bit):
+    value = value.reshape((2, -1) + value.shape[1:])
+    return pick(value, bit), low(pick(value, 1 - bit))
+
+
+def next_half(kept, got, bit):
+    kept = kept.reshape((2, -1) + kept.shape[1:])
+    got = got.reshape(kept.shape)
+    total = lambda at: pick(kept, at) + pick(got, at).astype(f32)
+    return total(bit), low(total(1 - bit))
+
+
+def reversed_bits(z):
+    bits = z_bits()
+    return sum(((z // bit) % 2) * back for bit, back in zip(bits, reversed(bits)))
 
 
 def norm_parts(values):
@@ -153,6 +153,12 @@
         scratch[pl.ds(at, rows), :] = part[...]
 
 
+def cost(microseconds):
+    return pl.CostEstimate(
+        flops=int(microseconds * 1e9), transcendentals=0, bytes_accessed=int(microseconds * 3e6)
+    )
+
+
 def params():
     return pltpu.CompilerParams(vmem_limit_bytes=VMEM_LIMIT)
 
@@ -161,38 +167,30 @@
 IN_VMEM = pl.BlockSpec(memory_space=pltpu.VMEM)
 
 
-def prepare_kernel(index_ref, qkv_ref, in_ref, *outs):
-    shard = index_ref[0]
-    width = qkv_ref.shape[1] // 12
-    ff = in_ref.shape[1] // 8
+def prepare_kernel(order, index_ref, w_ref, *outs):
+    part = w_ref.shape[1] // (4 * len(order))
     for s in range(4):
 
-        @pl.when(shard == s)
+        @pl.when(index_ref[0] == s)
         def _():
             for e in range(4):
                 t = s ^ SLOT_SHARD[e]
-                for place, third in enumerate((1, 2, 0)):
-                    at = third * 4 * width + t * width
-                    outs[e][:, place * width : (place + 1) * width] = qkv_ref[:, at : at + width]
-                for half in range(2):
-                    at = half * 4 * ff + t * ff
-                    outs[4 + e][:, half * ff : (half + 1) * ff] = in_ref[:, at : at + ff]
-
-
-def prepare(index, w_qkv, w_in):
-    rows = w_qkv.shape[0]
-    shapes = [jax.ShapeDtypeStruct((rows, w_qkv.shape[1] // 4), bf16)] * 4
-    shapes += [jax.ShapeDtypeStruct((rows, w_in.shape[1] // 4), bf16)] * 4
-    whole = pl.BlockSpec(memory_space=pltpu.VMEM)
-    got = pl.pallas_call(
-        prepare_kernel,
-        out_shape=shapes,
-        in_specs=[pl.BlockSpec(memory_space=pltpu.SMEM), whole, whole],
-        out_specs=[whole] * 8,
-        compiler_params=pltpu.CompilerParams(vmem_limit_bytes=VMEM_LIMIT),
+                for place, third in enumerate(order):
+                    at = (third * 4 + t) * part
+                    outs[e][:, place * part : (place + 1) * part] = w_ref[:, at : at + part]
+
+
+def prepare(index, weight, order):
+    shape = jax.ShapeDtypeStruct((weight.shape[0], weight.shape[1] // 4), bf16)
+    return pl.pallas_call(
+        functools.partial(prepare_kernel, order),
+        out_shape=[shape] * 4,
+        in_specs=[IN_SMEM, IN_VMEM],
+        out_specs=[IN_VMEM] * 4,
+        compiler_params=params(),
         name="prepare",
-    )(index, w_qkv, w_in)
-    return got[:4], got[4:]
+        cost_estimate=cost(2.4),
+    )(index, weight)
 
 
 def attend_kernel(q_ref, kv_ref, attn_ref, low_ref, lse_ref, max_ref, sum_ref, acc_ref):
@@ -255,6 +253,7 @@
         ],
         compiler_params=pltpu.CompilerParams(vmem_limit_bytes=VMEM_LIMIT),
         name="attend",
+        cost_estimate=cost(8.4),
     )(query, kv)
 
 
@@ -352,6 +351,7 @@
         ],
         compiler_params=params(),
         name="attend_back",
+        cost_estimate=cost(18),
     )(query, kv, *still, *bases, *q_bases, *row_tables)
 
 
@@ -421,6 +421,7 @@
         scratch_shapes=[pltpu.VMEM((features, cols), bf16)],
         compiler_params=params(),
         name="project",
+        cost_estimate=cost(7.5),
     )(index, a_all, b_all, *bases, *row_tables, gain, *weights)
 
 
@@ -500,6 +501,7 @@
         scratch_shapes=[pltpu.VMEM((features, 2 * ff), bf16), pltpu.VMEM((features, ff), bf16)],
         compiler_params=params(),
         name="middle_part",
+        cost_estimate=cost(8.6),
     )(index, a_all, b_all, *others)
 
 
@@ -528,6 +530,7 @@
         ],
         compiler_params=params(),
         name="branch",
+        cost_estimate=cost(3),
     )(half_sum, from_x, mid, cot[0], cot[1], gain)
 
 
@@ -589,7 +592,92 @@
         scratch_shapes=[pltpu.VMEM((features, cols), bf16)],
         compiler_params=params(),
         name="tokens_back",
+        cost_estimate=cost(4.5),
     )(index, d_kv, d_query, a_all, b_all, *weights)
+
+
+def chunk_row(index_ref, dy, offset, count, lead):
+    chunk = (index_ref[1] ^ dy) * count + (index_ref[2] ^ offset)
+    return pl.multiple_of(chunk * lead, lead)
+
+
+def place_columns_kernel(parts, offsets, index_ref, own_ref, got_ref, out_ref):
+    count, slots, lead, cols = own_ref.shape
+    part = cols // parts
+    for s in range(4):
+
+        @pl.when(index_ref[0] == s)
+        def _():
+            for dy, ref in enumerate((own_ref, got_ref)):
+                for j in range(count):
+                    rows = pl.ds(chunk_row(index_ref, dy, offsets[j], count, lead), lead)
+                    for e in range(slots):
+                        t = s ^ SLOT_SHARD[e]
+                        block = ref[j, e].astype(f32)
+                        for p in range(parts):
+                            at = (p * 4 + t) * part
+                            out_ref[rows, at : at + part] = block[:, p * part : (p + 1) * part]
+
+
+def place_rows_kernel(offsets, index_ref, own_ref, got_ref, first_ref, second_ref):
+    count = own_ref.shape[0]
+    lead = second_ref.shape[0] // (2 * count)
+    first = own_ref.shape[1] - lead
+    total = first_ref.shape[0]
+    for dy, ref in enumerate((own_ref, got_ref)):
+        for j in range(count):
+            block = ref[j].astype(f32)
+            at = chunk_row(index_ref, dy, offsets[j], count, first)
+            second_ref[pl.ds(chunk_row(index_ref, dy, offsets[j], count, lead), lead), :] = block[
+                first:
+            ]
+
+            @pl.when(at + first <= total)
+            def _():
+                first_ref[pl.ds(at, first), :] = block[:first]
+
+            if total % first:
+
+                @pl.when(at == total - total % first)
+                def _():
+                    first_ref[total - total % first :, :] = block[: total % first]
+
+
+def place(kernel, index, own, got, shapes):
+    return pl.pallas_call(
+        kernel,
+        in_specs=[IN_SMEM, IN_VMEM, IN_VMEM],
+        out_specs=[IN_VMEM] * len(shapes),
+        out_shape=[jax.ShapeDtypeStruct(shape, f32) for shape in shapes],
+        compiler_params=params(),
+        name="place",
+        cost_estimate=cost(2.6),
+    )(index, own, got)
+
+
+def finish_kernel(near_ref, got_ref, a_ref, b_ref, grad_ref, gain_ref, out_ref):
+    own = a_ref.shape[1]
+    for dy, ref in enumerate((a_ref, b_ref)):
+        rows = slice(dy * own, (dy + 1) * own)
+        grad_normed = near_ref[rows, :] + got_ref[rows, :].astype(f32)
+        xhat, inv = norm_parts(ref[0].astype(f32))
+        grad = grad_ref[rows, :] + norm_back(grad_normed, gain_ref[...], xhat, inv)
+        out_ref[rows, :] = low(grad)
+
+
+def finish(near, got, a_all, b_all, grad_middle, gain, rows):
+    features = gain.shape[1]
+    own = pl.BlockSpec((1, rows, features), lambda i: (0, 0, 0))
+    return pl.pallas_call(
+        finish_kernel,
+        grid=(1,),
+        in_specs=[IN_VMEM, IN_VMEM, own, own, IN_VMEM, IN_VMEM],
+        out_specs=IN_VMEM,
+        out_shape=jax.ShapeDtypeStruct((2 * rows, features), bf16),
+        compiler_params=params(),
+        name="finish",
+        cost_estimate=cost(2.4),
+    )(near, got, a_all, b_all, grad_middle, gain)
 
 
 def local(tokens, gain_attn, gain_ffn, w_qkv, w_attn, w_in, w_out, cotangent):
@@ -605,37 +693,45 @@
     ff = w_out.shape[0]
     w_rows = w_qkv.shape[0]
     slot_of = jnp.take(jnp.array(SLOT_SHARD), jnp.arange(shards) ^ shard)
-    index = jnp.stack([shard, y_index]).astype(jnp.int32)
-
-    both = jnp.stack([tokens, cotangent], axis=1)
-    mine, theirs = pick(both, y_index), pick(both, 1 - y_index)
-    got = swap(theirs, "y")
-
-    def gather_all(piece):
+    index = jnp.stack([shard, y_index, reversed_bits(z_index)]).astype(jnp.int32)
+
+    a_piece = pick(tokens, y_index)
+    b_piece = swap(pick(tokens, 1 - y_index), "y")
+
+    def gather_z(piece):
         piece = piece[None]
         for bit in reversed(z_bits()):
             piece = jnp.concatenate([piece, swap_z(piece, bit)])
-        piece = jnp.concatenate([piece, swap(piece, "x")])
+        return piece
+
+    def gather_core(piece, from_x):
+        piece = jnp.concatenate([piece, from_x])
         piece = jnp.concatenate([piece, swap(piece, "core")])
         return piece.reshape(shards, z_count * rows, features)
 
-    qkv_parts, in_parts = prepare(index, w_qkv, w_in)
-    a_all = gather_all(mine[0])
-    qkv_parts = exchange_shard(qkv_parts)
-    b_all = gather_all(got[0])
-    cot = gather_shard(jnp.concatenate([mine[1], got[1]]))
-    in_parts = exchange_shard(in_parts)
-    attn_parts = gather_shard(w_attn)
+    qkv_parts = exchange_shard(prepare(index, w_qkv, (1, 2, 0)))
+    a_column = gather_z(a_piece)
+    a_from_x = swap(a_column, "x")
+    b_column = gather_z(b_piece)
+    b_from_x = swap(after(b_column, qkv_parts[1:]), "x")
+    a_all, b_all = gather_core(a_column, a_from_x), gather_core(b_column, b_from_x)
+
+    w_in_late, w_attn_late, cot_late = after((w_in, w_attn, cotangent), b_from_x)
+    cot_own = pick(cot_late, y_index)
+    cot_own = jnp.concatenate([cot_own, swap(pick(cot_late, 1 - y_index), "y")])
+    in_parts = exchange_shard(prepare(index, w_in_late, (0, 1)))
+    late = (w_attn_late, cot_own)
+    late_x, late_core = [swap(v, "x") for v in late], [swap(v, "core") for v in late]
     gain_a, gain_f = gain_attn.reshape(1, features), gain_ffn.reshape(1, features)
 
     z_of = (z_index ^ jnp.array(z_offsets()))[None, None, :]
     s_of = (shard ^ jnp.array(SLOT_SHARD))[:, None, None]
     y_of = (y_index ^ jnp.arange(2))[None, :, None]
-    place = ((2 * z_of + y_of) * shards + s_of) * rows
+    starts = ((2 * z_of + y_of) * shards + s_of) * rows
     inverse_freq = jnp.exp(
         (jnp.arange(128) % HALF).astype(f32) * (-1.0 / HALF) * jnp.log(jnp.float32(rope_base))
     )
-    base_angles = place[..., None].astype(f32) * inverse_freq
+    base_angles = starts[..., None].astype(f32) * inverse_freq
     row_angles = jnp.arange(rows, dtype=f32)[:, None] * inverse_freq
     bases = (jnp.cos(base_angles), jnp.sin(base_angles))
     row_tables = (jnp.cos(row_angles), jnp.sin(row_angles))
@@ -645,7 +741,12 @@
 
     normed_a, kv, query = project(index, a_all, b_all, slot_bases, row_tables, gain_a, qkv_parts)
     query = query.reshape(group, width)
-    attn, attn_low, lse = attend(query, kv.reshape(-1, 2 * width))
+    attn, attn_low, lse = attend(after(query, in_parts[1:]), kv.reshape(-1, 2 * width))
+    attn_low = after(attn_low, late_x, late_core)
+    attn_parts, cot = (
+        [own, x, core, swap(after(x, lse), "core")]
+        for own, x, core in zip(late, late_x, late_core)
+    )
 
     got_attn = gather_shard(attn_low)
     send, keep, send_o, keep_o, mid, normed_f, hidden, grad_gate_up, gain_f_part = middle_part(
@@ -653,76 +754,193 @@
     )
 
     half_sum = keep + swap(send, "core").astype(f32)
-    half_branch, grad_middle = branch(half_sum, swap(low(half_sum), "x"), mid, cot, gain_f)
+    half_low = low(half_sum)
+    from_x = swap(half_low, "x")
+
+    def by_block(grad):
+        lead = w_rows // (2 * z_count)
+        return grad.reshape(shards, 2 * z_count, lead, -1).transpose(1, 0, 2, 3)
+
+    normed_f, grad_gate_up, hidden = after((normed_f, grad_gate_up, hidden), half_low)
+    in_kept, in_sent = first_half(by_block(dot_tn(normed_f, grad_gate_up)), y_index)
+    in_got = swap(in_sent, "y")
+    d_out = dot_tn(hidden, jnp.concatenate(cot))
+    out_lead = 8 * pl.cdiv(ff, 16 * z_count)
+
+    mid = after(mid, in_sent)
+    half_branch, grad_middle = branch(half_sum, from_x, mid, cot, gain_f)
     other = swap(half_branch, "core")
+
+    bits = z_bits()
+    z_bit = lambda bit: (z_index // bit) % 2
+    in_got = after(in_got, half_branch)
+    in_kept, in_sent = next_half(in_kept, in_got, z_bit(bits[0]))
+    in_got = swap_z(in_sent, bits[0])
+    d_attn = dot_tn(attn_low, jnp.concatenate([half_branch, other]))
+    rows_grad = jnp.concatenate(
+        [
+            jnp.pad(d_out, ((0, 2 * z_count * out_lead - ff), (0, 0))).reshape(
+                2 * z_count, out_lead, features
+            ),
+            d_attn.reshape(2 * z_count, -1, features),
+        ],
+        axis=1,
+    )
+    rows_kept, rows_sent = first_half(rows_grad, y_index)
+    rows_got = swap(rows_sent, "y")
+    out_got = swap(send_o, "core")
+    kv_late = after(kv, rows_sent, in_sent)
+
     d_kv, d_query = attend_back(
-        query, kv.reshape(-1, 2 * width), half_branch, other, w_attn, attn, lse,
+        query, kv_late.reshape(-1, 2 * width), half_branch, other, w_attn, attn, lse,
         flat_bases, q_bases, row_tables,
     )
+    turn_of = [d_query]
+
+    def step(function, *values):
+        values = after(values, turn_of[0])
+        result = function(*values)
+        turn_of[0] = result[-1] if isinstance(result, tuple) else result
+        return result
+
+    def z_step(kept, got, bit):
+        kept, sent = step(lambda k, g: next_half(k, g, z_bit(bit)), kept, got)
+        return kept, swap_z(sent, bit)
+
+    def total(kept, got):
+        return step(lambda k, g: low(k[0] + g[0].astype(f32)), kept, got)
+
+    def to_owners(value):
+        parts = [pick(value, shard ^ SLOT_SHARD[e]) for e in range(4)]
+        return jnp.stack(exchange_shard(parts))
+
+    def z_spread(value, bit):
+        return step(lambda v, g: jnp.concatenate([v, g]), value, swap_z(value, bit))
+
+    def token_step(kept, got, exchange):
+        def add(k, g):
+            k = k.reshape((2, -1) + k.shape[1:])
+            g = g.reshape(k.shape)
+            return k[0] + g[0].astype(f32), low(k[1] + g[1].astype(f32))
+
+        kept, sent = step(add, kept, got)
+        return kept, exchange(sent)
 
     d_kv_slots = d_kv.reshape(kv.shape)
     d_query_slots = d_query.reshape(shards, tok, width)
-    back = lambda first, dtype: tokens_back(
-        index, first, d_kv_slots, d_query_slots, a_all, b_all, qkv_parts, rows, dtype
-    )
-    far, gain_far = back(2, bf16)
-    near, gain_near = back(0, bf16)
-    near = near.astype(f32) + swap(far, "core").astype(f32)
-    near = near[0] + swap(low(near[1]), "x").astype(f32)
-    for bit in z_bits():
-        near = near.reshape((2, -1) + near.shape[1:])
-        near = near[0] + swap_z(low(near[1]), bit).astype(f32)
-    own = near.reshape(tok, features)
-    gain_a_part = gain_far + gain_near
-
-    grad_branch = jnp.concatenate([half_branch, other])
-    d_in = dot_tn(normed_f, grad_gate_up)
-    d_out = dot_tn(hidden, jnp.concatenate(cot))
-    d_attn = dot_tn(attn_low, grad_branch)
-    own_normed = normed_a[:, :, :rows].reshape(group, features)
-    d_qkv = jnp.concatenate(
-        [dot_tn(own_normed, d_query), dot_tn(normed_a.reshape(-1, features), d_kv)], axis=1
-    )
-
-    xhat_own, inv_own = norm_parts(jnp.concatenate([a_all[0, :rows], b_all[0, :rows]]).astype(f32))
-    grad_tokens = grad_middle + norm_back(own, gain_attn, xhat_own, inv_own)
-    out_near = keep_o + swap(send_o, "core").astype(f32)
-    out_own = out_near[:tok] + swap(low(out_near[tok:]), "x").astype(f32)
-    results = low(jnp.stack([out_own, grad_tokens])).reshape(2, 2, rows, features)
-    from_y = swap(results[:, 1], "y")
-    output = pair_in_order(results[0, 0], from_y[0], y_index)
-    grad_tokens = pair_in_order(results[1, 0], from_y[1], y_index)
-
-    def from_columns(grad, thirds):
-        lead = w_rows // (2 * z_count)
-        cut = grad.reshape(shards, 2 * z_count, lead, -1).transpose(1, 0, 2, 3)
-        total = low(ctx_sum(cut, z_index, y_index))
-        parts = exchange_shard([pick(total, shard ^ SLOT_SHARD[e]) for e in range(4)])
-        parts = jnp.take(jnp.stack(parts), slot_of, axis=0)
-        parts = parts.reshape(shards, lead, thirds, -1).transpose(1, 2, 0, 3).reshape(lead, -1)
-        return ctx_gather(parts, z_index, y_index).reshape(w_rows, -1).astype(f32)
-
-    rows_grad = jnp.concatenate([d_out, d_attn])
-    rows_grad = jnp.pad(rows_grad, ((0, -rows_grad.shape[0] % (2 * z_count)), (0, 0)))
-    rows_grad = rows_grad.reshape(2 * z_count, -1, features)
-    rows_grad = ctx_gather(low(ctx_sum(rows_grad, z_index, y_index)), z_index, y_index)
-    rows_grad = rows_grad.reshape(-1, features).astype(f32)
-
-    gains = jnp.concatenate([gain_a_part, gain_f_part])
-    for axis in ("core", "x", "y"):
-        gains = gains + swap(gains, axis)
-    for bit in z_bits():
-        gains = gains + swap_z(gains, bit)
+    back = lambda first, d, dtype: tokens_back(
+        index, first, d, d_query_slots, a_all, b_all, qkv_parts, rows, dtype
+    )
+    d_kv_slots = after(d_kv_slots, out_got)
+    far, gain_far = back(2, d_kv_slots, bf16)
+    turn_of[0] = gain_far
+    far = swap(far, "core")
+    out_near, out_sent = step(
+        lambda k, g: (k[:tok] + g[:tok].astype(f32), low(k[tok:] + g[tok:].astype(f32))),
+        keep_o, out_got,
+    )
+    out_x = swap(out_sent, "x")
+    for bit in bits[1:]:
+        in_kept, in_got = z_step(in_kept, in_got, bit)
+    rows_kept, rows_got = z_step(rows_kept, rows_got, bits[0])
+
+    def own_grads(all_normed, grad_kv, grad_q):
+        own = all_normed[:, :, :rows].reshape(group, features)
+        grads = [dot_tn(own, grad_q), dot_tn(all_normed.reshape(-1, features), grad_kv)]
+        return first_half(by_block(jnp.concatenate(grads, axis=1)), y_index)
+
+    qkv_kept, qkv_sent = step(own_grads, normed_a, d_kv, d_query)
+    qkv_got = swap(qkv_sent, "y")
+    near, gain_near = back(0, after(d_kv_slots, turn_of[0]), f32)
+    turn_of[0] = gain_near
+    gains = jnp.concatenate([gain_far + gain_near, gain_f_part])
+    gains_got = swap(gains, "core")
+
+    def gain_step(exchange):
+        summed = step(lambda k, g: k + g, gains, gains_got)
+        return summed, exchange(summed)
+
+    near, near_got = token_step(near, far, lambda v: swap(v, "x"))
+    near, near_got = (v.reshape((z_count,) + v.shape[-3:]) for v in (near, near_got))
+    output = step(lambda k, g: low(k + g.astype(f32)), out_near, out_x)
+    output = output.reshape(2, rows, features)
+    output_got = swap(output[1], "y")
+    for bit in bits[1:]:
+        rows_kept, rows_got = z_step(rows_kept, rows_got, bit)
+    in_all = to_owners(total(in_kept, in_got))[None]
+    qkv_kept, qkv_got = z_step(qkv_kept, qkv_got, bits[0])
+    gains, gains_got = gain_step(lambda v: swap(v, "x"))
+    for bit in reversed(bits[1:]):
+        in_all = z_spread(in_all, bit)
+    for bit in bits[1:]:
+        qkv_kept, qkv_got = z_step(qkv_kept, qkv_got, bit)
+    near, near_got = token_step(near, near_got, lambda v: swap_z(v, bits[0]))
+    rows_all = total(rows_kept, rows_got)[None]
+    gains, gains_got = gain_step(lambda v: swap(v, "y"))
+    qkv_all = to_owners(total(qkv_kept, qkv_got))[None]
+    for bit in bits[1:]:
+        near, near_got = token_step(near, near_got, lambda v: swap_z(v, bit))
+    in_all = z_spread(in_all, bits[0])
+    in_y = swap(in_all, "y")
+    for bit in reversed(bits[1:]):
+        qkv_all = z_spread(qkv_all, bit)
+        rows_all = z_spread(rows_all, bit)
+    gains, gains_got = gain_step(lambda v: swap_z(v, bits[0]))
+    near, near_got = after((near, near_got), turn_of[0])
+    grad_tokens = finish(
+        near.reshape(tok, features), near_got.reshape(tok, features), a_all, b_all,
+        grad_middle, gain_a, rows,
+    )
+    grad_tokens = grad_tokens.reshape(2, rows, features)
+    grad_got = swap(grad_tokens[1], "y")
+    turn_of[0] = grad_tokens
+    qkv_all = z_spread(qkv_all, bits[0])
+    qkv_y = swap(qkv_all, "y")
+    rows_all = z_spread(rows_all, bits[0])
+    rows_y = swap(rows_all, "y")
+    for bit in bits[1:]:
+        gains, gains_got = gain_step(lambda v: swap_z(v, bit))
+    gains = step(lambda k, g: k + g, gains, gains_got)
+    output = pair_in_order(output[0], output_got, y_index)
+    grad_tokens = pair_in_order(grad_tokens[0], grad_got, y_index)
+
+    lead = w_rows // (2 * z_count)
+    offsets = [reversed_bits(o) for o in z_offsets()]
+    if lead % 8 == 0:
+
+        def place_columns(own, got, parts):
+            kernel = functools.partial(place_columns_kernel, parts, offsets)
+            return place(kernel, index, own, got, [(w_rows, shards * own.shape[-1])])[0]
+
+        d_out, d_attn = place(
+            functools.partial(place_rows_kernel, offsets),
+            index, rows_all, rows_y, [(ff, features), (w_rows, features)],
+        )
+    else:
+        at_z = jnp.array(offsets) ^ index[2]
+        chunk = jnp.concatenate([y_index * z_count + at_z, (1 - y_index) * z_count + at_z])
+        ordered = lambda own, got: jnp.take(
+            jnp.concatenate([own, got]), jnp.argsort(chunk), axis=0
+        )
+
+        def place_columns(own, got, parts):
+            whole = jnp.take(ordered(own, got), slot_of, axis=1)
+            whole = whole.reshape(2 * z_count, shards, lead, parts, -1).transpose(0, 2, 3, 1, 4)
+            return whole.reshape(w_rows, -1).astype(f32)
+
+        whole = ordered(rows_all, rows_y)
+        d_out = whole[:, :out_lead].reshape(-1, features)[:ff].astype(f32)
+        d_attn = whole[:, out_lead:].reshape(-1, features).astype(f32)
 
     return (
         output,
         grad_tokens,
         gains[0],
         gains[1],
-        from_columns(d_qkv, 3),
-        rows_grad[ff : ff + w_rows],
-        from_columns(d_in, 2),
-        rows_grad[:ff],
+        place_columns(qkv_all, qkv_y, 3),
+        d_attn,
+        place_columns(in_all, in_y, 2),
+        d_out,
     )
 
 

time: 305 us -> 254 us (0.83)
  waiting for transfers between devices: 130 us -> 73 us
  starting transfers between devices: 51.6 us -> 64.7 us
  Pallas kernels: 58.3 us -> 70.3 us
  other arithmetic: 26.7 us -> 18.1 us
  local copies, waits for them, and re-layouts: 27.8 us -> 22.2 us
  matrix products: 7.75 us -> 3.43 us
    ppermute x39 -> x41, waiting for transfers between devices: 66.9 us -> 39.8 us  [swap(): return lax.ppermute(v, axis, [(0, 1), (1, 0)])]
    ppermute x20, waiting for transfers between devices: 57.5 us -> 33 us  [swap_z(): return lax.ppermute(v, 'z', [(i, i ^ bit) for i in range(count)])]
    pallas_call x1 -> x6, Pallas kernels: 3.26 us -> 15 us  [the longest x3 7.82 us: place(): pl.pallas_call(kernel, in_specs=[IN_SMEM, IN_VMEM, IN_VMEM], out_specs=[I...]
    ppermute x20, starting transfers between devices: 21.7 us -> 29 us  [swap_z(): return lax.ppermute(v, 'z', [(i, i ^ bit) for i in range(count)])]
    unnamed x127 -> x120, local copies, waits for them, and re-layouts: 5.74 us -> 12.7 us
    ppermute x39 -> x41, starting transfers between devices: 27.3 us -> 33.6 us  [swap(): return lax.ppermute(v, axis, [(0, 1), (1, 0)])]
    ppermute x4, waiting for transfers between devices: 5.54 us -> 0.13 us  [across(): return lax.ppermute(v, ('x', 'core'), [(i, 3 - i) for i in range(4)])]
    slice x7 -> x3, local copies, waits for them, and re-layouts: 5.34 us -> 0.08 us  [the longest x1 0.05 us: own_grads(): own = all_normed[:, :, :rows].reshape(group, features)]
  transfers between devices with their start and end apart: 63 -> 65, of which waited for: 29 -> 27; matrix products, arithmetic and copies ran while one was open for 16% -> 14% of each run, Pallas kernels for 6% -> 22%
where the time goes in v2:
time: 254 us; the launch traced here: 253 us
  waiting for transfers between devices  73 us (29%)
  Pallas kernels  70.3 us (28%)
  starting transfers between devices  64.7 us (25%)
  local copies, waits for them, and re-layouts  22.2 us (9%)
  other arithmetic  18.1 us (7%)
  matrix products  3.43 us (1%)
    ppermute x41, waiting for transfers between devices, swap(): return lax.ppermute(v, axis, [(0, 1), (1, 0)])  39.8 us
    ppermute x41, starting transfers between devices, swap(): return lax.ppermute(v, axis, [(0, 1), (1, 0)])  33.6 us
    ppermute x20, waiting for transfers between devices, swap_z(): return lax.ppermute(v, 'z', [(i, i ^ bit) for i in range(count)])  33 us
    ppermute x20, starting transfers between devices, swap_z(): return lax.ppermute(v, 'z', [(i, i ^ bit) for i in range(count)])  29 us
    pallas_call x1, Pallas kernels, attend_back(): pl.pallas_call(attend_back_kernel, grid=(kv.shape[0] // chunk,), in_specs...  18.4 us
    unnamed x120, local copies, waits for them, and re-layouts  12.7 us
    pallas_call x2, Pallas kernels, tokens_back(): pl.pallas_call(tokens_back_kernel, grid=(2,), in_specs=[IN_SMEM, pl.Block...  9.13 us
    pallas_call x1, Pallas kernels, attend(): pl.pallas_call(attend_kernel, grid=(kv.shape[0] // chunk,), in_specs=[fix...  8.52 us
  transfers between devices with their start and end apart: 65, of which 27 were waited for; matrix products, arithmetic and copies ran while one was open for 14% of the time, Pallas kernels for 22%

profile of v2, /device:TPU:0, one launch (start us, length us, event | category | flops | bytes accessed | tf_op | source)
XLA Modules:
  0.0 253.3 jit_solution(10586033523192858299)
XLA Ops:
  1.3 2.4 prepare.2
  3.7 3.0 %collective-permute-start.7 = (bf16[192,576]{1,0:T(8,128)(2,1)}, bf16[192,576]{1,0:T(8,128)(2,1)S(1)}, u32[]{:S(2)}, u32[]{:S(2)}) collective-permute-start(bf16[192,576]{1,0:T(8,128)(2,1)} %get-tuple-element.110), channel_id=1, source_target_pairs={{0,16},{16,0},{1,17},{17,1},{2,18},{18,2},{3,19},{19,3},{4,20},{20... | collective-permute-start | bytes 663560 | tf_op jit(solution)/shard_map/ppermute | solution.py:27
  9.5 2.6 %collective-permute-start = (bf16[1,64,768]{2,1,0:T(8,128)(2,1)S(1)}, bf16[1,64,768]{2,1,0:T(8,128)(2,1)S(1)}, u32[]{:S(2)}, u32[]{:S(2)}) collective-permute-start(bf16[1,64,768]{2,1,0:T(8,128)(2,1)S(1)} %get-tuple-element.219), channel_id=1, source_target_pairs={{0,4},{2,6},{4,0},{6,2},{1,5},{3,7},{5,1},{7,3},{8,12},{10,14},{12... | collective-permute-start | bytes 294920 | tf_op jit(solution)/shard_map/ppermute | solution.py:32
  16.9 2.9 %collective-permute-start.1 = (bf16[2,64,768]{2,1,0:T(8,128)(2,1)S(1)}, bf16[2,64,768]{2,1,0:T(8,128)(2,1)S(1)}, u32[]{:S(2)}, u32[]{:S(2)}) collective-permute-start(bf16[2,64,768]{2,1,0:T(8,128)(2,1)S(1)} %pad_maximum_fusion.5), channel_id=1, source_target_pairs={{0,2},{2,0},{4,6},{6,4},{1,3},{3,1},{5,7},{7,5},{8,10},{10,8},{12,... | collective-permute-start | bytes 589832 | tf_op jit(solution)/shard_map/ppermute | solution.py:32
  22.8 3.4 %collective-permute-done.1 = bf16[2,64,768]{2,1,0:T(8,128)(2,1)S(1)} collective-permute-done((bf16[2,64,768]{2,1,0:T(8,128)(2,1)S(1)}, bf16[2,64,768]{2,1,0:T(8,128)(2,1)S(1)}, u32[]{:S(2)}, u32[]{:S(2)}) %collective-permute-start.1) | collective-permute-done | bytes 196640 | tf_op jit(solution)/shard_map/ppermute | solution.py:32
  31.9 6.2 %collective-permute-done.2 = bf16[4,64,768]{2,1,0:T(8,128)(2,1)S(1)} collective-permute-done((bf16[4,64,768]{2,1,0:T(8,128)(2,1)S(1)}, bf16[4,64,768]{2,1,0:T(8,128)(2,1)S(1)}, u32[]{:S(2)}, u32[]{:S(2)}) %collective-permute-start.2) | collective-permute-done | bytes 393248 | tf_op jit(solution)/shard_map/ppermute | solution.py:27
  39.1 3.8 %collective-permute-done.10 = bf16[4,64,768]{2,1,0:T(8,128)(2,1)S(1)} collective-permute-done((bf16[4,64,768]{2,1,0:T(8,128)(2,1)S(1)}, bf16[4,64,768]{2,1,0:T(8,128)(2,1)S(1)}, u32[]{:S(2)}, u32[]{:S(2)}) %collective-permute-start.10) | collective-permute-done | bytes 393248 | tf_op jit(solution)/shard_map/ppermute | solution.py:27
  45.6 2.5 prepare.3
  54.2 7.5 %project.1 = (bf16[4,2,256,768]{3,2,1,0:T(8,128)(2,1)}, bf16[4,2,256,384]{3,2,1,0:T(8,128)(2,1)}, bf16[4,128,192]{2,1,0:T(8,128)(2,1)}) custom-call(s32[3]{0:T(128)} %pad_add_fusion.index_ref, bf16[4,256,768]{2,1,0:T(8,128)(2,1)} %bitcast.3.a_ref, bf16[4,256,768]{2,1,0:T(8,128)(2,1)} %bitcast.141, f32[4,8,128]{2,1,0:T(8,128)} %get-tuple-element.256.base_cos, ...), custom_call_target="tpu_custom_call" | custom-call | flops 7500000256 | bytes 22500000 | tf_op jit(solution)/shard_map/project/pallas_call | solution.py:407
  62.5 8.5 %attend.1 = (f32[512,192]{1,0:T(8,128)}, bf16[512,192]{1,0:T(8,128)(2,1)}, f32[512,128]{1,0:T(8,128)}) custom-call(bf16[512,192]{1,0:T(8,128)(2,1)} %bitcast.153, bf16[2048,384]{1,0:T(8,128)(2,1)} %bitcast.149), custom_call_target="tpu_custom_call" | custom-call | flops 8400000000 | bytes 25200000 | tf_op jit(solution)/shard_map/attend/pallas_call | solution.py:239
  73.9 5.9 %collective-permute-done.20.t1 = bf16[512,192]{1,0:T(8,128)(2,1)S(1)} collective-permute-done((bf16[512,192]{1,0:T(8,128)(2,1)}, bf16[512,192]{1,0:T(8,128)(2,1)S(1)}, u32[]{:S(2)}, u32[]{:S(2)}) %collective-permute-start.20) | collective-permute-done | bytes 196640 | tf_op jit(solution)/shard_map/ppermute | solution.py:27
  82.0 8.5 %middle_part.1 = (bf16[256,768]{1,0:T(8,128)(2,1)}, f32[256,768]{1,0:T(8,128)}, bf16[256,768]{1,0:T(8,128)(2,1)}, f32[256,768]{1,0:T(8,128)}, f32[256,768]{1,0:T...) custom-call(s32[3]{0:T(128)} %pad_add_fusion.index_ref, ...), custom_call_target="tpu_custom_call" | custom-call | flops 8600000512 | bytes 25800000 | tf_op jit(solution)/shard_map/middle_part/pallas_call | solution.py:495
  98.4 7.9 %collective-permute-done.27.x_ref = bf16[256,768]{1,0:T(8,128)(2,1)S(1)} collective-permute-done((bf16[256,768]{1,0:T(8,128)(2,1)S(1)}, bf16[256,768]{1,0:T(8,128)(2,1)S(1)}, u32[]{:S(2)}, u32[]{:S(2)}) %collective-permute-start.27) | collective-permute-done | bytes 393248 | tf_op jit(solution)/shard_map/ppermute | solution.py:27
  107.0 3.2 %branch.1 = (bf16[256,768]{1,0:T(8,128)(2,1)}, f32[128,768]{1,0:T(8,128)}) custom-call(f32[256,768]{1,0:T(8,128)} %get-tuple-element.217.half_ref, bf16[256,768]{1,0:T(8,128)(2,1)} %copy-done.34, f32[256,768]{1,0:T(8,128)} %get-tuple-element.141.mid_ref, bf16[128,768]{1,0:T(8,128)(2,1)} %copy-done.12, bf16[128,768]{1,0:T(8,128)(2,1)} %copy-done.13, ...), custom_call_target="tpu_custom_call" | custom-call | flops 3000000000 | bytes 9000000 | tf_op jit(solution)/shard_map/branch/pallas_call | solution.py:523
  113.7 18.4 %attend_back.1 = (bf16[2048,384]{1,0:T(8,128)(2,1)}, bf16[512,192]{1,0:T(8,128)(2,1)}) custom-call(bf16[512,192]{1,0:T(8,128)(2,1)} %bitcast.154, bf16[2048,384]{1,0:T(8,128)(2,1)} %bitcast.150, bf16[256,768]{1,0:T(8,128)(2,1)} %get-tuple-element.142.half_ref, bf16[256,768]{1,0:T(8,128)(2,1)} %copy-done.32, bf16[192,768]{1,0:T(8,128)(2,1)} %w_ref.4, ...), custom_call_target="tpu_custom_call" | custom-call | flops 17999998976 | bytes 54000000 | tf_op jit(solution)/shard_map/attend_back/pallas_call | solution.py:333
  132.1 4.5 %tokens_back.2 = (bf16[2,4,2,64,768]{4,3,2,1,0:T(8,128)(2,1)}, f32[1,768]{1,0:T(1,128)}) custom-call(s32[3]{0:T(128)} %pad_add_fusion.index_ref, bf16[4,2,256,384]{3,2,1,0:T(8,128)(2,1)} %bitcast.151, bf16[4,128,192]{2,1,0:T(8,128)(2,1)} %bitcast.130, bf16[4,256,768]{2,1,0:T(8,128)(2,1)} %bitcast.3.a_ref, bf16[4,256,768]{2,1,0:T(8,128)(2,1)} %bitcast.143, ...), custom_call_target="tpu_custom_call" | custom-call | flops 4499999744 | bytes 13500000 | tf_op jit(solution)/shard_map/tokens_back/pallas_call | solution.py:573
  139.6 4.1 %collective-permute-start.38 = (bf16[1,4,24,576]{3,2,1,0:T(8,128)(2,1)}, bf16[1,4,24,576]{3,2,1,0:T(8,128)(2,1)}, u32[]{:S(2)}, u32[]{:S(2)}) collective-permute-start(bf16[1,4,24,576]{3,2,1,0:T(8,128)(2,1)} %get-tuple-element.237), channel_id=1, source_target_pairs={{0,4},{2,6},{4,0},{6,2},{1,5},{3,7},{5,1},{7,3},{8,12},{10,14},{12... | collective-permute-start | bytes 331784 | tf_op jit(solution)/shard_map/ppermute | solution.py:32
  153.5 4.6 %tokens_back.3 = (f32[2,4,2,64,768]{4,3,2,1,0:T(8,128)}, f32[1,768]{1,0:T(1,128)}) custom-call(s32[3]{0:T(128)} %pad_add_fusion.index_ref, bf16[4,2,256,384]{3,2,1,0:T(8,128)(2,1)} %bitcast.152, bf16[4,128,192]{2,1,0:T(8,128)(2,1)} %bitcast.131, bf16[4,256,768]{2,1,0:T(8,128)(2,1)} %bitcast.3.a_ref, bf16[4,256,768]{2,1,0:T(8,128)(2,1)} %bitcast.144, ...), custom_call_target="tpu_custom_call" | custom-call | flops 4499999744 | bytes 13500000 | tf_op jit(solution)/shard_map/tokens_back/pallas_call | solution.py:573
  159.0 3.2 %add_bitcast_fusion = (f32[4,2,64,768]{3,2,1,0:T(8,128)S(1)}, bf16[1,4,2,64,768]{4,3,2,1,0:T(8,128)(2,1)}) fusion(f32[2,4,2,64,768]{4,3,2,1,0:T(8,128)} %get-tuple-element.164, bf16[2,4,2,64,768]{4,3,2,1,0:T(8,128)(2,1)S(1)} %collective-permute-done.33), kind=kLoop, calls=%fused_computation.5 | loop fusion | flops 1966080 | bytes 7077888 | tf_op jit(solution)/shard_map/reshape | solution.py:864
  178.8 2.8 %collective-permute-done.37 = bf16[2,4,24,576]{3,2,1,0:T(8,128)(2,1)S(1)} collective-permute-done((bf16[2,4,24,576]{3,2,1,0:T(8,128)(2,1)}, bf16[2,4,24,576]{3,2,1,0:T(8,128)(2,1)S(1)}, u32[]{:S(2)}, u32[]{:S(2)}) %collective-permute-start.37) | collective-permute-done | bytes 221216 | tf_op jit(solution)/shard_map/ppermute | solution.py:32
  183.7 5.4 %collective-permute-done.51 = bf16[1,4,24,576]{3,2,1,0:T(8,128)(2,1)S(1)} collective-permute-done((bf16[1,4,24,576]{3,2,1,0:T(8,128)(2,1)S(1)}, bf16[1,4,24,576]{3,2,1,0:T(8,128)(2,1)S(1)}, u32[]{:S(2)}, u32[]{:S(2)}) %collective-permute-start.51) | collective-permute-done | bytes 110624 | tf_op jit(solution)/shard_map/ppermute | solution.py:32
  190.7 2.7 %collective-permute-done.35 = bf16[1,4,2,64,768]{4,3,2,1,0:T(8,128)(2,1)S(1)} collective-permute-done((bf16[1,4,2,64,768]{4,3,2,1,0:T(8,128)(2,1)S(1)}, bf16[1,4,2,64,768]{4,3,2,1,0:T(8,128)(2,1)S(1)}, u32[]{:S(2)}, u32[]{:S(2)}) %collective-permute-start.35) | collective-permute-done | bytes 786464 | tf_op jit(solution)/shard_map/ppermute | solution.py:27
  196.8 2.9 %collective-permute-start.49 = (bf16[1,64,768]{2,1,0:T(8,128)(2,1)S(1)}, bf16[1,64,768]{2,1,0:T(8,128)(2,1)S(1)}, u32[]{:S(2)}, u32[]{:S(2)}) collective-permute-start(bf16[1,64,768]{2,1,0:T(8,128)(2,1)S(1)} %copy-done.22), channel_id=1, source_target_pairs={{0,4},{2,6},{4,0},{6,2},{1,5},{3,7},{5,1},{7,3},{8,12},{10,14},{12... | collective-permute-start | bytes 294920 | tf_op jit(solution)/shard_map/ppermute | solution.py:32
  200.9 6.8 %collective-permute-done.49 = bf16[1,64,768]{2,1,0:T(8,128)(2,1)S(1)} collective-permute-done((bf16[1,64,768]{2,1,0:T(8,128)(2,1)S(1)}, bf16[1,64,768]{2,1,0:T(8,128)(2,1)S(1)}, u32[]{:S(2)}, u32[]{:S(2)}) %collective-permute-start.49) | collective-permute-done | bytes 98336 | tf_op jit(solution)/shard_map/ppermute | solution.py:32
  207.7 3.5 %collective-permute-start.50 = (bf16[1,64,768]{2,1,0:T(8,128)(2,1)S(1)}, bf16[1,64,768]{2,1,0:T(8,128)(2,1)S(1)}, u32[]{:S(2)}, u32[]{:S(2)}) collective-permute-start(bf16[1,64,768]{2,1,0:T(8,128)(2,1)S(1)} %add_convert_fusion.12), channel_id=1, source_target_pairs={{0,4},{2,6},{4,0},{6,2},{1,5},{3,7},{5,1},{7,3},{8,12},{10,14},{12... | collective-permute-start | bytes 294920 | tf_op jit(solution)/shard_map/ppermute | solution.py:32
  214.8 3.9 %collective-permute-done.56 = bf16[2,4,24,576]{3,2,1,0:T(8,128)(2,1)S(1)} collective-permute-done((bf16[2,4,24,576]{3,2,1,0:T(8,128)(2,1)S(1)}, bf16[2,4,24,576]{3,2,1,0:T(8,128)(2,1)S(1)}, u32[]{:S(2)}, u32[]{:S(2)}) %collective-permute-start.56) | collective-permute-done | bytes 221216 | tf_op jit(solution)/shard_map/ppermute | solution.py:32
  222.7 2.3 finish.1
  228.4 2.5 collective-permute-start.61
  238.1 2.7 %place.5 = f32[192,2304]{1,0:T(8,128)} custom-call(s32[3]{0:T(128)} %pad_add_fusion.index_ref, bf16[4,4,24,576]{3,2,1,0:T(8,128)(2,1)} %copy-done.19, bf16[4,4,24,576]{3,2,1,0:T(8,128)(2,1)} %copy-done.29), custom_call_target="tpu_custom_call" | custom-call | flops 2600000000 | bytes 7800000 | tf_op jit(solution)/shard_map/place/pallas_call | solution.py:647
  240.9 3.7 %collective-permute-done.63.got_ref = bf16[4,64,768]{2,1,0:T(8,128)(2,1)S(1)} collective-permute-done((bf16[4,64,768]{2,1,0:T(8,128)(2,1)S(1)}, bf16[4,64,768]{2,1,0:T(8,128)(2,1)S(1)}, u32[]{:S(2)}, u32[]{:S(2)}) %collective-permute-start.63) | collective-permute-done | bytes 393248 | tf_op jit(solution)/shard_map/ppermute | solution.py:27
  245.3 2.4 place.4
  250.6 2.7 %place.3 = f32[192,2304]{1,0:T(8,128)} custom-call(s32[3]{0:T(128)} %pad_add_fusion.index_ref, bf16[4,4,24,576]{3,2,1,0:T(8,128)(2,1)} %copy-done.20, bf16[4,4,24,576]{3,2,1,0:T(8,128)(2,1)} %copy-done.30), custom_call_target="tpu_custom_call" | custom-call | flops 2600000000 | bytes 7800000 | tf_op jit(solution)/shard_map/place/pallas_call | solution.py:647
  (314 shorter events, 104.2 us)
Async XLA Ops:
  3.7 25.3 %collective-permute-start.7 = (bf16[192,576]{1,0:T(8,128)(2,1)}, bf16[192,576]{1,0:T(8,128)(2,1)S(1)}, u32[]{:S(2)}, u32[]{:S(2)}) collective-permute-start(bf16[192,576]{1,0:T(8,128)(2,1)} %get-tuple-element.110), channel_id=1, source_target_pairs={{0,16},{16,0},{1,17},{17,1},{2,18},{18,2},{3,19},{19,3},{4,20},{20... | collective-permute-start | bytes 663560 | tf_op jit(solution)/shard_map/ppermute | solution.py:27
  6.6 22.4 %collective-permute-start.8 = (bf16[192,576]{1,0:T(8,128)(2,1)}, bf16[192,576]{1,0:T(8,128)(2,1)S(1)}, u32[]{:S(2)}, u32[]{:S(2)}) collective-permute-start(bf16[192,576]{1,0:T(8,128)(2,1)} %get-tuple-element.111), channel_id=1, source_target_pairs={{0,8},{8,0},{1,9},{9,1},{2,10},{10,2},{3,11},{11,3},{4,12},{12,4},... | collective-permute-start | bytes 663560 | tf_op jit(solution)/shard_map/ppermute | solution.py:27
  6.6 23.1 %collective-permute-start.9 = (bf16[192,576]{1,0:T(8,128)(2,1)}, bf16[192,576]{1,0:T(8,128)(2,1)S(1)}, u32[]{:S(2)}, u32[]{:S(2)}) collective-permute-start(bf16[192,576]{1,0:T(8,128)(2,1)} %get-tuple-element.112), channel_id=1, source_target_pairs={{0,24},{8,16},{16,8},{24,0},{1,25},{9,17},{17,9},{25,1},{2,26},{10... | collective-permute-start | bytes 663560 | tf_op jit(solution)/shard_map/ppermute | solution.py:36
  26.2 11.9 %collective-permute-start.2 = (bf16[4,64,768]{2,1,0:T(8,128)(2,1)S(1)}, bf16[4,64,768]{2,1,0:T(8,128)(2,1)S(1)}, u32[]{:S(2)}, u32[]{:S(2)}) collective-permute-start(bf16[4,64,768]{2,1,0:T(8,128)(2,1)S(1)} %pad_maximum_fusion.3), channel_id=1, source_target_pairs={{0,16},{16,0},{1,17},{17,1},{2,18},{18,2},{3,19},{19,3},{4,20},{20... | collective-permute-start | bytes 1179656 | tf_op jit(solution)/shard_map/ppermute | solution.py:27
  29.7 13.2 %collective-permute-start.10 = (bf16[4,64,768]{2,1,0:T(8,128)(2,1)S(1)}, bf16[4,64,768]{2,1,0:T(8,128)(2,1)S(1)}, u32[]{:S(2)}, u32[]{:S(2)}) collective-permute-start(bf16[4,64,768]{2,1,0:T(8,128)(2,1)S(1)} %pad_maximum_fusion.4), channel_id=1, source_target_pairs={{0,16},{16,0},{1,17},{17,1},{2,18},{18,2},{3,19},{19,3},{4,20},{20... | collective-permute-start | bytes 1179656 | tf_op jit(solution)/shard_map/ppermute | solution.py:27
  38.2 12.2 %collective-permute-start.3 = (bf16[8,64,768]{2,1,0:T(8,128)(2,1)S(1)}, bf16[8,64,768]{2,1,0:T(8,128)(2,1)S(1)}, u32[]{:S(2)}, u32[]{:S(2)}) collective-permute-start(bf16[8,64,768]{2,1,0:T(8,128)(2,1)S(1)} %pad_maximum_fusion.1), channel_id=1, source_target_pairs={{0,8},{8,0},{1,9},{9,1},{2,10},{10,2},{3,11},{11,3},{4,12},{12,4},... | collective-permute-start | bytes 2359304 | tf_op jit(solution)/shard_map/ppermute | solution.py:27
  42.9 28.1 %collective-permute-start.18 = (bf16[192,768]{1,0:T(8,128)(2,1)S(1)}, bf16[192,768]{1,0:T(8,128)(2,1)S(1)}, u32[]{:S(2)}, u32[]{:S(2)}) collective-permute-start(bf16[192,768]{1,0:T(8,128)(2,1)S(1)} %copy-done.35), channel_id=1, source_target_pairs={{0,8},{8,0},{1,9},{9,1},{2,10},{10,2},{3,11},{11,3},{4,12},{12,4},... | collective-permute-start | bytes 884744 | tf_op jit(solution)/shard_map/ppermute | solution.py:27
  42.9 28.1 %collective-permute-start.15 = (bf16[192,768]{1,0:T(8,128)(2,1)S(1)}, bf16[192,768]{1,0:T(8,128)(2,1)}, u32[]{:S(2)}, u32[]{:S(2)}) collective-permute-start(bf16[192,768]{1,0:T(8,128)(2,1)S(1)} %copy-done.35), channel_id=1, source_target_pairs={{0,16},{16,0},{1,17},{17,1},{2,18},{18,2},{3,19},{19,3},{4,20},{20... | collective-permute-start | bytes 884744 | tf_op jit(solution)/shard_map/ppermute | solution.py:27
  49.8 11.9 %collective-permute-start.12 = (bf16[192,576]{1,0:T(8,128)(2,1)}, bf16[192,576]{1,0:T(8,128)(2,1)S(1)}, u32[]{:S(2)}, u32[]{:S(2)}) collective-permute-start(bf16[192,576]{1,0:T(8,128)(2,1)} %get-tuple-element.117), channel_id=1, source_target_pairs={{0,16},{16,0},{1,17},{17,1},{2,18},{18,2},{3,19},{19,3},{4,20},{20... | collective-permute-start | bytes 663560 | tf_op jit(solution)/shard_map/ppermute | solution.py:27
  50.4 11.4 %collective-permute-start.13 = (bf16[192,576]{1,0:T(8,128)(2,1)}, bf16[192,576]{1,0:T(8,128)(2,1)S(1)}, u32[]{:S(2)}, u32[]{:S(2)}) collective-permute-start(bf16[192,576]{1,0:T(8,128)(2,1)} %get-tuple-element.118), channel_id=1, source_target_pairs={{0,8},{8,0},{1,9},{9,1},{2,10},{10,2},{3,11},{11,3},{4,12},{12,4},... | collective-permute-start | bytes 663560 | tf_op jit(solution)/shard_map/ppermute | solution.py:27
  51.4 11.1 %collective-permute-start.14 = (bf16[192,576]{1,0:T(8,128)(2,1)S(1)}, bf16[192,576]{1,0:T(8,128)(2,1)S(1)}, u32[]{:S(2)}, u32[]{:S(2)}) collective-permute-start(bf16[192,576]{1,0:T(8,128)(2,1)S(1)} %copy-done.48), channel_id=1, source_target_pairs={{0,24},{8,16},{16,8},{24,0},{1,25},{9,17},{17,9},{25,1},{2,26},{10... | collective-permute-start | bytes 663560 | tf_op jit(solution)/shard_map/ppermute | solution.py:36
  93.7 38.4 %collective-permute-start.25 = (bf16[256,768]{1,0:T(8,128)(2,1)}, bf16[256,768]{1,0:T(8,128)(2,1)S(1)}, u32[]{:S(2)}, u32[]{:S(2)}) collective-permute-start(bf16[256,768]{1,0:T(8,128)(2,1)} %get-tuple-element.131), channel_id=1, source_target_pairs={{0,8},{8,0},{1,9},{9,1},{2,10},{10,2},{3,11},{11,3},{4,12},{12,4},... | collective-permute-start | bytes 1179656 | tf_op jit(solution)/shard_map/ppermute | solution.py:27
  95.1 11.2 %collective-permute-start.27 = (bf16[256,768]{1,0:T(8,128)(2,1)S(1)}, bf16[256,768]{1,0:T(8,128)(2,1)S(1)}, u32[]{:S(2)}, u32[]{:S(2)}) collective-permute-start(bf16[256,768]{1,0:T(8,128)(2,1)S(1)} %get-tuple-element.216), channel_id=1, source_target_pairs={{0,16},{16,0},{1,17},{17,1},{2,18},{18,2},{3,19},{19,3},{4,20},{20... | collective-permute-start | bytes 1179656 | tf_op jit(solution)/shard_map/ppermute | solution.py:27
  97.6 13.1 %collective-permute-start.29 = (bf16[4,4,24,576]{3,2,0,1:T(8,128)(2,1)S(1)}, bf16[4,4,24,576]{3,2,0,1:T(8,128)(2,1)S(1)}, u32[]{:S(2)}, u32[]{:S(2)}) collective-permute-start(bf16[4,4,24,576]{3,2,0,1:T(8,128)(2,1)S(1)} %fusion.8), channel_id=1, source_target_pairs={{0,1},{1,0},{2,3},{3,2},{4,5},{5,4},{6,7},{7,6},{8,9},{9,8},{10,11... | collective-permute-start | bytes 1327112 | tf_op jit(solution)/shard_map/ppermute | solution.py:27
  111.0 27.9 %collective-permute-start.32 = (bf16[2,4,24,576]{3,2,1,0:T(8,128)(2,1)S(1)}, bf16[2,4,24,576]{3,2,1,0:T(8,128)(2,1)S(1)}, u32[]{:S(2)}, u32[]{:S(2)}) collective-permute-start(bf16[2,4,24,576]{3,2,1,0:T(8,128)(2,1)S(1)} %get-tuple-element.227), channel_id=1, source_target_pairs={{0,2},{2,0},{4,6},{6,4},{1,3},{3,1},{5,7},{7,5},{8,10},{10,8},{12,... | collective-permute-start | bytes 663560 | tf_op jit(solution)/shard_map/ppermute | solution.py:32
  112.9 30.9 %collective-permute-start.31 = (bf16[4,64,768]{2,1,0:T(8,128)(2,1)S(1)}, bf16[4,64,768]{2,1,0:T(8,128)(2,1)S(1)}, u32[]{:S(2)}, u32[]{:S(2)}) collective-permute-start(bf16[4,64,768]{2,1,0:T(8,128)(2,1)S(1)} %fusion.10), channel_id=1, source_target_pairs={{0,1},{1,0},{2,3},{3,2},{4,5},{5,4},{6,7},{7,6},{8,9},{9,8},{10,11... | collective-permute-start | bytes 1179656 | tf_op jit(solution)/shard_map/ppermute | solution.py:27
  137.4 24.8 %collective-permute-start.30 = (bf16[128,768]{1,0:T(8,128)(2,1)S(1)}, bf16[128,768]{1,0:T(8,128)(2,1)}, u32[]{:S(2)}, u32[]{:S(2)}) collective-permute-start(bf16[128,768]{1,0:T(8,128)(2,1)S(1)} %get-tuple-element.232), channel_id=1, source_target_pairs={{0,16},{16,0},{1,17},{17,1},{2,18},{18,2},{3,19},{19,3},{4,20},{20... | collective-permute-start | bytes 589832 | tf_op jit(solution)/shard_map/ppermute | solution.py:27
  139.6 25.2 %collective-permute-start.38 = (bf16[1,4,24,576]{3,2,1,0:T(8,128)(2,1)}, bf16[1,4,24,576]{3,2,1,0:T(8,128)(2,1)}, u32[]{:S(2)}, u32[]{:S(2)}) collective-permute-start(bf16[1,4,24,576]{3,2,1,0:T(8,128)(2,1)} %get-tuple-element.237), channel_id=1, source_target_pairs={{0,4},{2,6},{4,0},{6,2},{1,5},{3,7},{5,1},{7,3},{8,12},{10,14},{12... | collective-permute-start | bytes 331784 | tf_op jit(solution)/shard_map/ppermute | solution.py:32
  143.7 15.2 %collective-permute-start.33 = (bf16[2,4,2,64,768]{4,3,2,1,0:T(8,128)(2,1)}, bf16[2,4,2,64,768]{4,3,2,1,0:T(8,128)(2,1)S(1)}, u32[]{:S(2)}, u32[]{:S(2)}) collective-permute-start(bf16[2,4,2,64,768]{4,3,2,1,0:T(8,128)(2,1)} %get-tuple-element.162), channel_id=1, source_target_pairs={{0,8},{8,0},{1,9},{9,1},{2,10},{10,2},{3,11},{11,3},{4,12},{12,4},... | collective-permute-start | bytes 4718600 | tf_op jit(solution)/shard_map/ppermute | solution.py:27
  144.7 18.5 %collective-permute-start.39 = (bf16[2,64,768]{2,1,0:T(8,128)(2,1)}, bf16[2,64,768]{2,1,0:T(8,128)(2,1)}, u32[]{:S(2)}, u32[]{:S(2)}) collective-permute-start(bf16[2,64,768]{2,1,0:T(8,128)(2,1)} %get-tuple-element.231), channel_id=1, source_target_pairs={{0,2},{2,0},{4,6},{6,4},{1,3},{3,1},{5,7},{7,5},{8,10},{10,8},{12,... | collective-permute-start | bytes 589832 | tf_op jit(solution)/shard_map/ppermute | solution.py:32
  152.0 16.2 %collective-permute-start.36 = (bf16[4,4,24,576]{3,2,0,1:T(8,128)(2,1)S(1)}, bf16[4,4,24,576]{3,2,0,1:T(8,128)(2,1)}, u32[]{:S(2)}, u32[]{:S(2)}) collective-permute-start(bf16[4,4,24,576]{3,2,0,1:T(8,128)(2,1)S(1)} %fusion.9), channel_id=1, source_target_pairs={{0,1},{1,0},{2,3},{3,2},{4,5},{5,4},{6,7},{7,6},{8,9},{9,8},{10,11... | collective-permute-start | bytes 1327112 | tf_op jit(solution)/shard_map/ppermute | solution.py:27
  175.1 46.6 %collective-permute-start.48 = (f32[2,768]{1,0:T(2,128)S(1)}, f32[2,768]{1,0:T(2,128)S(1)}, u32[]{:S(2)}, u32[]{:S(2)}) collective-permute-start(f32[2,768]{1,0:T(2,128)S(1)} %add.350), channel_id=1, source_target_pairs={{0,1},{1,0},{2,3},{3,2},{4,5},{5,4},{6,7},{7,6},{8,9},{9,8},{10,11... | collective-permute-start | bytes 18440 | tf_op jit(solution)/shard_map/ppermute | solution.py:27
  175.7 17.7 %collective-permute-start.35 = (bf16[1,4,2,64,768]{4,3,2,1,0:T(8,128)(2,1)S(1)}, bf16[1,4,2,64,768]{4,3,2,1,0:T(8,128)(2,1)S(1)}, u32[]{:S(2)}, u32[]{:S(2)}) collective-permute-start(bf16[1,4,2,64,768]{4,3,2,1,0:T(8,128)(2,1)S(1)} %copy-done.4), channel_id=1, source_target_pairs={{0,16},{16,0},{1,17},{17,1},{2,18},{18,2},{3,19},{19,3},{4,20},{20... | collective-permute-start | bytes 2359304 | tf_op jit(solution)/shard_map/ppermute | solution.py:27
  183.1 11.9 %collective-permute-start.34 = (bf16[64,768]{1,0:T(8,128)(2,1)S(1)}, bf16[64,768]{1,0:T(8,128)(2,1)S(1)}, u32[]{:S(2)}, u32[]{:S(2)}) collective-permute-start(bf16[64,768]{1,0:T(8,128)(2,1)S(1)} %get-tuple-element.243), channel_id=1, source_target_pairs={{0,1},{1,0},{2,3},{3,2},{4,5},{5,4},{6,7},{7,6},{8,9},{9,8},{10,11... | collective-permute-start | bytes 294920 | tf_op jit(solution)/shard_map/ppermute | solution.py:27
  194.9 17.7 %collective-permute-start.45 = (bf16[2,2,64,768]{3,2,1,0:T(8,128)(2,1)S(1)}, bf16[2,2,64,768]{3,2,1,0:T(8,128)(2,1)S(1)}, u32[]{:S(2)}, u32[]{:S(2)}) collective-permute-start(bf16[2,2,64,768]{3,2,1,0:T(8,128)(2,1)S(1)} %get-tuple-element.222), channel_id=1, source_target_pairs={{0,2},{2,0},{4,6},{6,4},{1,3},{3,1},{5,7},{7,5},{8,10},{10,8},{12,... | collective-permute-start | bytes 1179656 | tf_op jit(solution)/shard_map/ppermute | solution.py:32
  196.8 11.0 %collective-permute-start.49 = (bf16[1,64,768]{2,1,0:T(8,128)(2,1)S(1)}, bf16[1,64,768]{2,1,0:T(8,128)(2,1)S(1)}, u32[]{:S(2)}, u32[]{:S(2)}) collective-permute-start(bf16[1,64,768]{2,1,0:T(8,128)(2,1)S(1)} %copy-done.22), channel_id=1, source_target_pairs={{0,4},{2,6},{4,0},{6,2},{1,5},{3,7},{5,1},{7,3},{8,12},{10,14},{12... | collective-permute-start | bytes 294920 | tf_op jit(solution)/shard_map/ppermute | solution.py:32
  199.7 19.0 %collective-permute-start.56 = (bf16[2,4,24,576]{3,2,1,0:T(8,128)(2,1)S(1)}, bf16[2,4,24,576]{3,2,1,0:T(8,128)(2,1)S(1)}, u32[]{:S(2)}, u32[]{:S(2)}) collective-permute-start(bf16[2,4,24,576]{3,2,1,0:T(8,128)(2,1)S(1)} %constant_dynamic-update-slice_fusion.15), channel_id=1, source_target_pairs={{0,2},{2,0},{4,6},{6,4},{1,3},{3,1},{5,7},{7,5},{8,10},{10,8},{12,... | collective-permute-start | bytes 663560 | tf_op jit(solution)/shard_map/ppermute | solution.py:32
  200.7 18.5 %collective-permute-start.55 = (bf16[1,4,24,576]{3,2,1,0:T(8,128)(2,1)S(1)}, bf16[1,4,24,576]{3,2,1,0:T(8,128)(2,1)S(1)}, u32[]{:S(2)}, u32[]{:S(2)}) collective-permute-start(bf16[1,4,24,576]{3,2,1,0:T(8,128)(2,1)S(1)} %maximum_bitcast_fusion.1), channel_id=1, source_target_pairs={{0,4},{2,6},{4,0},{6,2},{1,5},{3,7},{5,1},{7,3},{8,12},{10,14},{12... | collective-permute-start | bytes 331784 | tf_op jit(solution)/shard_map/ppermute | solution.py:32
  207.7 11.9 %collective-permute-start.50 = (bf16[1,64,768]{2,1,0:T(8,128)(2,1)S(1)}, bf16[1,64,768]{2,1,0:T(8,128)(2,1)S(1)}, u32[]{:S(2)}, u32[]{:S(2)}) collective-permute-start(bf16[1,64,768]{2,1,0:T(8,128)(2,1)S(1)} %add_convert_fusion.12), channel_id=1, source_target_pairs={{0,4},{2,6},{4,0},{6,2},{1,5},{3,7},{5,1},{7,3},{8,12},{10,14},{12... | collective-permute-start | bytes 294920 | tf_op jit(solution)/shard_map/ppermute | solution.py:32
  218.8 18.6 %collective-permute-start.64 = (bf16[4,4,24,576]{3,2,1,0:T(8,128)(2,1)S(1)}, bf16[4,4,24,576]{3,2,1,0:T(8,128)(2,1)S(1)}, u32[]{:S(2)}, u32[]{:S(2)}) collective-permute-start(bf16[4,4,24,576]{3,2,1,0:T(8,128)(2,1)S(1)} %constant_dynamic-update-slice_fusion.17.own_ref), channel_id=1, source_target_pairs={{0,1},{1,0},{2,3},{3,2},{4,5},{5,4},{6,7},{7,6},{8,9},{9,8},{10,11... | collective-permute-start | bytes 1327112 | tf_op jit(solution)/shard_map/ppermute | solution.py:27
  232.2 12.4 %collective-permute-start.63 = (bf16[4,64,768]{2,1,0:T(8,128)(2,1)S(1)}, bf16[4,64,768]{2,1,0:T(8,128)(2,1)S(1)}, u32[]{:S(2)}, u32[]{:S(2)}) collective-permute-start(bf16[4,64,768]{2,1,0:T(8,128)(2,1)S(1)} %constant_dynamic-update-slice_fusion.25.own_ref), channel_id=1, source_target_pairs={{0,1},{1,0},{2,3},{3,2},{4,5},{5,4},{6,7},{7,6},{8,9},{9,8},{10,11... | collective-permute-start | bytes 1179656 | tf_op jit(solution)/shard_map/ppermute | solution.py:27
  233.0 16.8 %collective-permute-start.62 = (bf16[4,4,24,576]{3,2,1,0:T(8,128)(2,1)S(1)}, bf16[4,4,24,576]{3,2,1,0:T(8,128)(2,1)S(1)}, u32[]{:S(2)}, u32[]{:S(2)}) collective-permute-start(bf16[4,4,24,576]{3,2,1,0:T(8,128)(2,1)S(1)} %constant_dynamic-update-slice_fusion.23.own_ref), channel_id=1, source_target_pairs={{0,1},{1,0},{2,3},{3,2},{4,5},{5,4},{6,7},{7,6},{8,9},{9,8},{10,11... | collective-permute-start | bytes 1327112 | tf_op jit(solution)/shard_map/ppermute | solution.py:27
  (84 other events, 478.7 us)
